TPU v7x, 512 devices: a whole 4x4x16 slice. The times are simulated.
512 devices in a mesh: tm: 8 (over x, core), pair: 64 (over z, y).
Axes of the slice: x: 4, y: 4, z: 16, core: 2. Of those that a mesh axis runs over, the one named last changes fastest.
Arguments:
- traces: float32 [16, 8192, 1024], P('tm', 'pair'), may hold values from -6 to 6
- owner: int32 [64], replicated, may hold values from 0 to 63, each once
- tiles: int32 [192, 2], P('pair'), may hold values from 0 to 63, as said below
- counts: int32 [64], P('pair'), may hold values from 1 to 3, as said below
Outputs:
- stacks: float32 [192, 128, 16384], P('pair', None, 'tm')
Inputs may be any that keep to these rules, and one draw needn't show every extreme that they name: `tiles`: each row names fiber blocks a <= b with b - a at most 6. `counts`: the first that many of an index's 3 slots are live; some index has all 3 live.
All inputs are finite; a program needn't handle non-finite values.
Results may differ from a plain program's by a relative error of at most 0.0038.
Values may be sent and summed in bfloat16 or wider, within the bound.
A program may use at most 64 MiB of HBM per device.

v0:
```python
import math

import jax
import jax.numpy as jnp
from jax import lax
from jax.sharding import PartitionSpec as P

NT = 1024
NF = 128
LOW_BIN = 8
LAGS = 128


def forward_table():
    samples = jnp.arange(NT, dtype=jnp.int32)
    bins = LOW_BIN + jnp.arange(NF, dtype=jnp.int32)
    phase = samples[:, None] * bins[None, :] % NT
    angle = phase.astype(jnp.float32) * (2.0 * math.pi / NT)
    return jnp.concatenate([jnp.cos(angle), -jnp.sin(angle)], axis=1)


def inverse_table():
    shifts = jnp.arange(LAGS, dtype=jnp.int32) - LAGS // 2
    bins = LOW_BIN + jnp.arange(NF, dtype=jnp.int32)
    phase = jnp.mod(shifts[:, None] * bins[None, :], NT)
    angle = phase.astype(jnp.float32) * (2.0 * math.pi / NT)
    return (jnp.cos(angle), -jnp.sin(angle))


def window_sum(values):
    widths = [(0, 0)] * (values.ndim - 1) + [(2, 2)]
    padded = jnp.pad(values, widths)
    total = padded[..., 0:NF]
    for offset in range(1, 5):
        total = total + padded[..., offset : offset + NF]
    return total


def whiten(spectrum):
    real_part = spectrum[..., :NF]
    imag_part = spectrum[..., NF:]
    power = real_part * real_part + imag_part * imag_part
    counted = window_sum(jnp.ones((NF,), jnp.float32))
    smooth = window_sum(power) / counted
    level = jnp.mean(power, axis=-1, keepdims=True)
    factor = lax.rsqrt(smooth + 0.05 * level + 1e-06)
    return jnp.concatenate([real_part * factor, imag_part * factor], axis=-1).astype(jnp.bfloat16)


def lookup(owner, fiber_ids):
    onehot = fiber_ids[..., None] == jnp.arange(owner.shape[0], dtype=jnp.int32)
    return jnp.sum(jnp.where(onehot, owner, 0), axis=-1)


def shards(traces, owner, tiles, counts):
    seg_count, block, samples = traces.shape
    rows = seg_count * block
    width = 2 * NF
    spectrum = jnp.dot(
        traces.reshape(rows, samples), forward_table(), precision=lax.Precision.HIGHEST
    )
    white = whiten(spectrum)
    time_count = lax.axis_size("tm")
    segments = seg_count * time_count
    share = block // time_count
    slots = tiles.shape[0]
    scale = 1.0 / math.sqrt(segments * NF)
    cos_part, sin_part = inverse_table()
    every = lax.all_gather(white[None], "pair", axis=0, tiled=True)
    stored = lookup(owner, tiles)
    picked = jnp.take(every, stored.reshape(-1), axis=0).reshape(slots, 2, rows, width)
    number = picked.shape[0]
    left = picked[:, 0].reshape(number, seg_count, block, width)
    right = picked[:, 1].reshape(number, seg_count, block, width)
    left_all = lax.all_to_all(left, "tm", split_axis=2, concat_axis=1, tiled=True)
    right_all = lax.all_gather(right, "tm", axis=1, tiled=True)
    left_real = left_all[..., :NF]
    left_imag = left_all[..., NF:]
    right_real = right_all[..., :NF]
    right_imag = right_all[..., NF:]
    cross_real = jnp.einsum(
        "qsif,qsjf->qfij", left_real, right_real, preferred_element_type=jnp.float32
    )
    cross_real = cross_real + jnp.einsum(
        "qsif,qsjf->qfij", left_imag, right_imag, preferred_element_type=jnp.float32
    )
    cross_imag = jnp.einsum(
        "qsif,qsjf->qfij", left_real, right_imag, preferred_element_type=jnp.float32
    )
    cross_imag = cross_imag - jnp.einsum(
        "qsif,qsjf->qfij", left_imag, right_real, preferred_element_type=jnp.float32
    )
    cross_real = cross_real.reshape(number, NF, share * block)
    cross_imag = cross_imag.reshape(number, NF, share * block)
    lagged = jnp.einsum("lf,qfx->qlx", cos_part, cross_real, precision=lax.Precision.HIGHEST)
    lagged = lagged + jnp.einsum(
        "lf,qfx->qlx", sin_part, cross_imag, precision=lax.Precision.HIGHEST
    )
    partial_value = lagged * scale
    live = (jnp.arange(slots, dtype=jnp.int32) < counts[0]).astype(jnp.float32)
    return partial_value * live[:, None, None]


def solution(mesh):
    placed = (P("tm", "pair", None), P(), P("pair", None), P("pair"))
    return jax.shard_map(
        shards, mesh=mesh, in_specs=placed, out_specs=P("pair", None, "tm"), check_vma=False
    )
```

profile of v0, /device:TPU:1, one launch (start us, length us, event | category | flops | bytes accessed | tf_op | source)
XLA Modules:
  0.0 259.8 jit_solution(12651376614939929892)
XLA Ops:
  6.6 2.1 fusion.9
  8.6 1.8 convolution_bitcast_fusion
  10.8 0.8 copy.56
  12.0 154.2 %all-gather.3.cloned.1.call-done = bf16[64,256,256]{2,1,0:T(8,128)(2,1)} async-done(((bf16[1,256,256]{2,1,0:T(8,128)(2,1)}), bf16[64,256,256]{2,1,0:T(8,128)(2,1)}) %all-gather.3.cloned.1.call-update) | async-done | bytes 8388624 | tf_op jit(solution)/shard_map/all_gather | solution.py:69
  166.3 4.0 %gather_fusion = bf16[6,256,256]{2,1,0:T(8,128)(2,1)S(1)} fusion(bf16[64,256,256]{2,1,0:T(8,128)(2,1)} %all-gather.3.cloned.1.call-done, s32[1024]{0:T(1024)S(1)} %pad_clamp_fusion), kind=kCustom, calls=%fused_computation | custom fusion | bytes 1572888 | tf_op jit(solution)/shard_map/jit(_take)/gather | solution.py:71
  170.5 0.8 copy.61
  171.3 1.2 copy.57
  172.4 12.6 %all-to-all-start = ((bf16[3,2,128,256]{3,1,0,2:T(2,128)(2,1)}), bf16[3,2,128,256]{3,1,0,2:T(2,128)(2,1)S(1)}, u32[]{:S(2)}, u32[]{:S(2)}) async-start(bf16[3,2,128,256]{3,1,0,2:T(2,128)(2,1)} %copy.57), calls=%async_computation | async-start | bytes 786432 | tf_op jit(solution)/shard_map/all_to_all | solution.py:75
  185.6 7.4 %all-to-all-done = bf16[3,2,128,256]{3,1,0,2:T(2,128)(2,1)S(1)} async-done(((bf16[3,2,128,256]{3,1,0,2:T(2,128)(2,1)}), bf16[3,2,128,256]{3,1,0,2:T(2,128)(2,1)S(1)}, u32[]{:S(2)}, u32[]{:S(2)}) %all-to-all-start) | async-done | bytes 393248 | tf_op jit(solution)/shard_map/all_to_all | solution.py:75
  193.2 1.7 copy.72
  194.9 1.1 copy.74
  196.0 13.7 %all-gather.5.cloned.1.call-done = bf16[3,16,128,256]{3,2,0,1:T(8,128)(2,1)} async-done(((bf16[3,2,128,256]{3,2,0,1:T(8,128)(2,1)}), bf16[3,16,128,256]{3,2,0,1:T(8,128)(2,1)}) %all-gather.5.cloned.1.call-update) | async-done | bytes 3145744 | tf_op jit(solution)/shard_map/all_gather | solution.py:76
  209.8 4.0 %fusion.39 = (bf16[3,16,128,128]{3,2,0,1:T(8,128)(2,1)}, bf16[3,16,128,128]{3,2,0,1:T(8,128)(2,1)}) fusion(bf16[3,16,128,256]{3,2,0,1:T(8,128)(2,1)} %all-gather.5.cloned.1.call-done), kind=kLoop, calls=%fused_computation.71 | loop fusion | bytes 6291456 | tf_op jit(solution)/shard_map/slice | solution.py:80
  213.7 2.8 %copy.75 = bf16[3,16,128,128]{2,1,3,0:T(8,128)(2,1)} copy(bf16[3,16,128,128]{3,2,0,1:T(8,128)(2,1)} %get-tuple-element.9) | data formatting | bytes 3145728
  216.5 2.8 %copy.73 = bf16[3,16,128,128]{2,1,3,0:T(8,128)(2,1)} copy(bf16[3,16,128,128]{3,2,0,1:T(8,128)(2,1)} %get-tuple-element.10) | data formatting | bytes 3145728
  219.3 3.0 %fusion.43 = f32[3,128,16,128]{3,2,1,0:T(8,128)S(1)} fusion(bf16[3,16,16,128]{1,2,3,0:T(8,128)(2,1)} %copy.72, bf16[3,16,128,128]{2,1,3,0:T(8,128)(2,1)} %copy.75), kind=kOutput, calls=%fused_computation.75 | convolution fusion | flops 25165824 | bytes 4915200 | tf_op jit(solution)/shard_map/qsif,qsjf->qfij/dot_general | solution.py:87
  222.3 2.6 %fusion.42 = f32[3,128,16,128]{3,2,1,0:T(8,128)} fusion(bf16[3,16,16,128]{1,2,3,0:T(8,128)(2,1)S(1)} %copy-done.1, bf16[3,16,128,128]{2,1,3,0:T(8,128)(2,1)S(1)} %copy-done.2), kind=kOutput, calls=%fused_computation.74 | convolution fusion | flops 25165824 | bytes 4915200 | tf_op jit(solution)/shard_map/qsif,qsjf->qfij/dot_general | solution.py:81
  225.0 2.6 %convolution_subtract_fusion = f32[3,128,16,128]{3,2,1,0:T(8,128)} fusion(f32[3,128,16,128]{3,2,1,0:T(8,128)S(1)} %fusion.43, bf16[3,16,16,128]{1,2,3,0:T(8,128)(2,1)S(1)} %copy.74, bf16[3,16,128,128]{2,1,3,0:T(8,128)(2,1)S(1)} %copy-done.2), kind=kOutput, calls=%fused_computation.2 | convolution fusion | flops 25952256 | bytes 8060928 | tf_op jit(solution)/shard_map/qsif,qsjf->qfij/dot_general | solution.py:90
  227.6 3.5 %copy.71 = f32[3,128,16,128]{1,3,2,0:T(8,128)} copy(f32[3,128,16,128]{3,2,1,0:T(8,128)} %convolution_subtract_fusion) | data formatting | bytes 6291456 | tf_op jit(solution)/shard_map/reshape | solution.py:94
  231.1 5.0 %convolution_add_fusion = f32[3,128,16,128]{3,2,1,0:T(8,128)} fusion(f32[3,128,16,128]{3,2,1,0:T(8,128)} %fusion.42, bf16[3,16,16,128]{1,2,3,0:T(8,128)(2,1)S(1)} %copy.74, bf16[3,16,128,128]{2,1,3,0:T(8,128)(2,1)} %copy.75), kind=kOutput, calls=%fused_computation.3 | convolution fusion | flops 25952256 | bytes 8060928 | tf_op jit(solution)/shard_map/qsif,qsjf->qfij/dot_general | solution.py:84
  236.1 3.6 %copy.70 = f32[3,128,16,128]{1,3,2,0:T(8,128)} copy(f32[3,128,16,128]{3,2,1,0:T(8,128)} %convolution_add_fusion) | data formatting | bytes 6291456 | tf_op jit(solution)/shard_map/reshape | solution.py:93
  239.7 5.0 %fusion.16 = f32[3,2048,128]{2,1,0:T(8,128)S(1)} fusion(f32[3,128,2048]{1,2,0:T(8,128)} %bitcast.41, s32[128]{0:T(128)S(1)} %get-tuple-element.18, s32[128]{0:T(128)S(1)} %get-tuple-element.17), kind=kOutput, calls=%fused_computation.37 | convolution fusion | flops 1208188928 | bytes 6292480 | tf_op jit(solution)/shard_map/lf,qfx->qlx/dot_general | solution.py:95
  244.7 4.7 %multiply_bitcast_fusion = f32[3,128,2048]{1,2,0:T(8,128)} fusion(f32[3,2048,128]{2,1,0:T(8,128)S(1)} %fusion.16, f32[3,128,2048]{1,2,0:T(8,128)S(1)} %bitcast.40, f32[3]{0:T(128)S(1)} %compare_select_fusion.3, s32[128]{0:T(128)S(1)} %get-tuple-element.18, s32[128]{0:T(128)S(1)} %get-tuple-element.17), kind=kOutput, calls=%fused_computation.1 | convolution fusion | flops 1209778176 | bytes 9438220 | tf_op jit(solution)/shard_map/lf,qfx->qlx/dot_general | solution.py:96
  249.4 3.5 %copy.67 = f32[3,128,2048]{2,1,0:T(8,128)} copy(f32[3,128,2048]{1,2,0:T(8,128)} %multiply_bitcast_fusion) | data formatting | bytes 6291456 | tf_op jit(solution)/shard_map/mul | solution.py:101
  (36 shorter events, 1.1 us)
Async XLA Ops:
  6.5 2.1 copy-start
  6.5 5.1 %copy-start.4 = (s32[3,2]{0,1:T(2,128)S(1)}, s32[3,2]{0,1:T(2,128)}, u32[]{:S(2)}) copy-start(s32[3,2]{0,1:T(2,128)} %param.6) | copy-start | bytes 76
  6.5 5.2 %copy-start.5 = (s32[64]{0:T(128)S(1)}, s32[64]{0:T(128)}, u32[]{:S(2)}) copy-start(s32[64]{0:T(128)} %param.5) | copy-start | bytes 772
  6.5 159.7 %all-gather.3.cloned.1.call-start = ((), (), s32[]{:S(2)}) async-start(), calls=%async_computation.1 | async-start | bytes 8519680 | tf_op jit(solution)/shard_map/all_gather | solution.py:69
  11.6 198.2 %all-gather.5.cloned.1.call-start = ((), (), s32[]{:S(2)}) async-start(), calls=%async_computation.2 | async-start | bytes 3538944 | tf_op jit(solution)/shard_map/all_gather | solution.py:76
  172.4 20.6 %all-to-all-start = ((bf16[3,2,128,256]{3,1,0,2:T(2,128)(2,1)}), bf16[3,2,128,256]{3,1,0,2:T(2,128)(2,1)S(1)}, u32[]{:S(2)}, u32[]{:S(2)}) async-start(bf16[3,2,128,256]{3,1,0,2:T(2,128)(2,1)} %copy.57), calls=%async_computation | async-start | bytes 786432 | tf_op jit(solution)/shard_map/all_to_all | solution.py:75
  219.3 3.0 %copy-start.1 = (bf16[3,16,16,128]{1,2,3,0:T(8,128)(2,1)S(1)}, bf16[3,16,16,128]{1,2,3,0:T(8,128)(2,1)}, u32[]{:S(2)}) copy-start(bf16[3,16,16,128]{1,2,3,0:T(8,128)(2,1)} %copy.72) | copy-start | bytes 589828
  219.3 3.0 %copy-start.2 = (bf16[3,16,128,128]{2,1,3,0:T(8,128)(2,1)S(1)}, bf16[3,16,128,128]{2,1,3,0:T(8,128)(2,1)}, u32[]{:S(2)}) copy-start(bf16[3,16,128,128]{2,1,3,0:T(8,128)(2,1)} %copy.73) | copy-start | bytes 4718596
  239.7 5.0 %copy-start.3 = (f32[3,128,16,128]{1,3,2,0:T(8,128)S(1)}, f32[3,128,16,128]{1,3,2,0:T(8,128)}, u32[]{:S(2)}) copy-start(f32[3,128,16,128]{1,3,2,0:T(8,128)} %copy.71) | copy-start | bytes 9437188
Sparse Core Ops, SparseCore 0:
  11.7 154.5 all-gather.2
  171.4 38.3 all-gather.4
where the time goes:
time: 260 us
  waiting for transfers between devices  175 us (67%)
  local copies, waits for them, and re-layouts  30.1 us (12%)
  matrix products  24.7 us (10%)
  between operations  14.2 us (5%)
  starting transfers between devices  12.6 us (5%)
  other arithmetic  2.73 us (1%)
    all_gather x1, waiting for transfers between devices, shards(): every = lax.all_gather(white[None], 'pair', axis=0, tiled=True)  154 us
    all_gather x1, waiting for transfers between devices, shards(): right_all = lax.all_gather(right, 'tm', axis=1, tiled=True)  13.7 us
    all_to_all x1, starting transfers between devices, shards(): lax.all_to_all(left, 'tm', split_axis=2, concat_axis=1, tiled=True)  12.6 us
    unnamed x17, local copies, waits for them, and re-layouts  8.55 us
    all_to_all x1, waiting for transfers between devices, shards(): lax.all_to_all(left, 'tm', split_axis=2, concat_axis=1, tiled=True)  7.41 us
  transfers between devices with their start and end apart: 3, of which 3 were waited for; matrix products, arithmetic and copies ran while one was open for 2% of the time, Pallas kernels for 0%

commit v1 on v0

v1 whole, which is shorter than its diff:
```python
import functools
import math

import jax
import jax.numpy as jnp
import ml_dtypes
import numpy as np
from jax import lax
from jax.experimental import pallas as pl
from jax.experimental.pallas import tpu as pltpu
from jax.sharding import PartitionSpec as P

BLOCK = 128
NT = 1024
NF = 128
LOW_BIN = 8
LAGS = 128
NG = 16
NZ = 16
NY = 4
NX = 4
NTM = 8
SLOTS = 3
UNITS = 2 * SLOTS
CHUNKS = 4
GC = NG // CHUNKS
BF = jnp.bfloat16
F32 = jnp.float32
MESH = pl.DeviceIdType.MESH


def split(table):
    high = table.astype(np.float32).astype(ml_dtypes.bfloat16)
    low = (table.astype(np.float32) - high.astype(np.float32)).astype(ml_dtypes.bfloat16)
    return high, low


def forward_table():
    samples = np.arange(NT)
    bins = LOW_BIN + np.arange(NF)
    angle = (bins[:, None] * samples[None, :] % NT) * (2.0 * math.pi / NT)
    return split(np.concatenate([np.cos(angle), -np.sin(angle)], axis=0))


def inverse_table():
    shifts = np.arange(LAGS) - LAGS // 2
    bins = LOW_BIN + np.arange(NF)
    angle = (shifts[:, None] * bins[None, :] % NT) * (2.0 * math.pi / NT)
    parts = np.stack([np.cos(angle), -np.sin(angle)], axis=0)
    parts = parts.reshape(2, LAGS, NG, 8).transpose(1, 2, 0, 3)
    return split(parts.reshape(LAGS, 2 * NF))


def nt_dot(a, b):
    return lax.dot_general(a, b, (((1,), (1,)), ((), ())), preferred_element_type=F32)


def exchange_kernel(
    traces, tab_hi, tab_lo, owner, tiles, b_out, p_out,
    slabs, picks, stage_a, stage_d, stage_m, got_x, got_p, got_m,
    packed, choose, req_v, req_s,
    z_send, z_recv, r_send, r_recv, r_loc, a_send, a_recv, d_send, d_recv, m_send, m_recv,
    b_send, b_recv, p_send, p_recv, own_sem,
):
    t = lax.axis_index("tm")
    pair = lax.axis_index("pair")
    z, y = pair // NY, pair % NY
    x, core = t // 2, t % 2

    def at_z(step):
        return {"pair": ((z + step + NZ) % NZ) * NY + y}

    def at_y(step):
        return {"pair": z * NY + (y + step + NY) % NY}

    def at_x(step):
        return {"tm": ((x + step + NX) % NX) * 2 + core}

    def at_t(step):
        return {"tm": (t + step) % NTM}

    sibling = {"tm": x * 2 + 1 - core}

    barrier = pltpu.get_barrier_semaphore()
    greet = [at_z(1), at_z(-1)] + [at_y(d) for d in (1, 2, 3)] + [at_t(d) for d in range(1, NTM)]
    for who in greet:
        pl.semaphore_signal(barrier, inc=1, device_id=who, device_id_type=MESH)

    values = traces[...]
    v_hi = values.astype(BF)
    v_lo = (values - v_hi.astype(F32)).astype(BF)
    spec = nt_dot(tab_hi[...], v_hi) + (nt_dot(tab_hi[...], v_lo) + nt_dot(tab_lo[...], v_hi))
    real, imag = spec[:NF], spec[NF:]
    power = real * real + imag * imag
    width = power.shape[1]
    bin_of = lax.broadcasted_iota(jnp.int32, power.shape, 0)
    total = power
    for step in (1, 2):
        ahead = pltpu.roll(power, NF - step, 0)
        behind = pltpu.roll(power, step, 0)
        total = total + jnp.where(bin_of < NF - step, ahead, 0.0)
        total = total + jnp.where(bin_of >= step, behind, 0.0)
    edge = jnp.minimum(jnp.minimum(bin_of, NF - 1 - bin_of), 2)
    smooth = total / (edge + 3).astype(F32)
    level = jnp.sum(power, axis=0, keepdims=True) * (1.0 / NF)
    factor = lax.rsqrt(smooth + 0.05 * level + 1e-06)
    white = jnp.concatenate(
        [(real * factor).reshape(NG, 8, width), (imag * factor).reshape(NG, 8, width)], axis=1
    ).astype(BF)
    slabs[z, :, 0] = white[:, :, :BLOCK]
    slabs[z, :, 1] = white[:, :, BLOCK:]

    mine = []
    lane = lax.broadcasted_iota(jnp.int32, (8, 128), 1)
    row = jnp.zeros((8, 128), jnp.int32)
    for u in range(UNITS):
        wanted = owner[tiles[u % SLOTS, u // SLOTS]]
        mine.append(wanted)
        row = jnp.where(lane == u, wanted, row)
    req_v[0] = row

    pl.semaphore_wait(barrier, len(greet))

    def z_copy(way, step, c):
        sign = 1 - 2 * way
        index = (z - sign * step + NZ) % NZ
        ref = slabs.at[index, pl.ds(c * GC, GC)]
        return pltpu.make_async_remote_copy(
            src_ref=ref, dst_ref=ref,
            send_sem=z_send.at[way, step, c], recv_sem=z_recv.at[way, step, c],
            device_id=at_z(sign), device_id_type=MESH,
        )

    def z_arrived(way, step, c):
        sign = 1 - 2 * way
        index = (z - sign * (step + 1) + NZ) % NZ
        ref = slabs.at[index, pl.ds(c * GC, GC)]
        pltpu.make_async_remote_copy(
            src_ref=ref, dst_ref=ref,
            send_sem=z_send.at[way, step, c], recv_sem=z_recv.at[way, step, c],
            device_id=at_z(sign), device_id_type=MESH,
        ).wait_recv()

    last = NZ // 2 - 1

    def z_pieces(step):
        for c in range(CHUNKS):
            for way in (0, 1):
                if step < last or (c < CHUNKS // 2) == (way == 0):
                    yield way, c

    z_started = []
    for way, c in z_pieces(0):
        copy = z_copy(way, 0, c)
        copy.start()
        z_started.append(copy)

    r_copies = []
    for d in (1, 2, 3):
        copy = pltpu.make_async_remote_copy(
            src_ref=req_v.at[0], dst_ref=req_v.at[d],
            send_sem=r_send.at[d], recv_sem=r_recv.at[d],
            device_id=at_y(d), device_id_type=MESH,
        )
        copy.start()
        r_copies.append(copy)

    r_i = lax.broadcasted_iota(jnp.int32, (BLOCK, BLOCK), 0)
    c_i = lax.broadcasted_iota(jnp.int32, (BLOCK, BLOCK), 1)
    for to in range(NTM):
        inside = (r_i >= 16 * to) & (r_i < 16 * to + 16)
        for part in range(UNITS):
            hit = inside & (c_i - r_i == 16 * part - 16 * to)
            choose[to, pl.ds(part * BLOCK, BLOCK), :] = jnp.where(hit, 1.0, 0.0).astype(BF)

    for copy in r_copies:
        copy.wait()
    for d in (1, 2, 3):
        local = pltpu.make_async_copy(req_v.at[d], req_s.at[d], r_loc.at[d])
        local.start()
        local.wait()

    for step in range(1, last + 1):
        for way, c in z_pieces(step):
            z_arrived(way, step - 1, c)
            copy = z_copy(way, step, c)
            copy.start()
            z_started.append(copy)
        if step == last:
            for c in range(CHUNKS):
                for way in (0, 1):
                    if (way, c) not in list(z_pieces(last)):
                        z_arrived(way, step - 1, c)
    for way, c in z_pieces(last):
        z_arrived(way, last, c)

    def asked(d, u):
        wanted = mine[u] if d == 0 else req_s[(NY - d) % NY, 0, u]
        return wanted // NY, wanted % NY

    def send(src, dst, s_sem, r_sem, who):
        copy = pltpu.make_async_remote_copy(
            src_ref=src, dst_ref=dst, send_sem=s_sem, recv_sem=r_sem,
            device_id=who, device_id_type=MESH,
        )
        copy.start()
        return copy

    copies = {}

    def first_hop(u):
        index, _ = asked(2, u)
        for s in (0, 1):
            stage_a[u, s] = slabs[index, :, s]
            copies["a", u, s] = send(
                stage_a.at[u, s], got_x.at[u, s], a_send.at[u, s], a_recv.at[u, s],
                at_y(1 if s == 0 else -1),
            )

    def direct(u):
        for s, d, got in ((1, 1, got_p), (0, -1, got_m)):
            index, _ = asked(d % NY, u)
            stage_d[u, s] = slabs[index, :, s]
            copies["d", u, s] = send(
                stage_d.at[u, s], got.at[u, s], d_send.at[u, s], d_recv.at[u, s], at_y(d)
            )

    def merged(u):
        for s, d, got in ((0, 1, got_p), (1, -1, got_m)):
            index, column = asked(d % NY, u)
            copies["a", u, s].wait_recv()
            stage_m[u, s] = jnp.where(column == y, slabs[index, :, s], got_x[u, s])
            copies["m", u, s] = send(
                stage_m.at[u, s], got.at[u, s], m_send.at[u, s], m_recv.at[u, s], at_y(d)
            )

    def finish(u):
        index, column = asked(0, u)
        for s in (0, 1):
            copies["d", u, s].wait_recv()
            copies["m", u, s].wait_recv()
        up, down = (y + 1) % NY, (y + NY - 1) % NY
        own = column == y
        first = jnp.where(column == up, got_m[u, 0], got_p[u, 0])
        picks[u, :, 0] = jnp.where(own, slabs[index, :, 0], first)
        second = jnp.where(column == down, got_p[u, 1], got_m[u, 1])
        picks[u, :, 1] = jnp.where(own, slabs[index, :, 1], second)

    def send_first():
        lanes = jnp.concatenate(
            [picks[u, :, s].reshape(2 * NF, BLOCK) for u in range(SLOTS) for s in (0, 1)], axis=1
        )
        for to in range(NTM):
            packed[to] = jnp.dot(lanes, choose[to], preferred_element_type=F32).astype(BF)
        for d in range(1, NTM):
            to = (t + d) % NTM
            copies["p", d] = send(
                packed.at[to], p_out.at[t], p_send.at[d], p_recv.at[d], at_t(d)
            )
        copies["p", 0] = pltpu.make_async_copy(packed.at[t], p_out.at[t], own_sem.at[SLOTS])
        copies["p", 0].start()

    half = NG // 2

    def t_of(step, c=None):
        return ((x + step + NX) % NX) * 2 + (core if c is None else c)

    def b_send_to(k, n, src, where, who):
        copies["b", k, n] = send(src, where, b_send.at[k, n], b_recv.at[k, n], who)

    def b_arrived(k, n, ref):
        pltpu.make_async_remote_copy(
            src_ref=ref, dst_ref=ref, send_sem=b_send.at[k, n], recv_sem=b_recv.at[k, n],
            device_id=sibling, device_id_type=MESH,
        ).wait_recv()

    def send_second(k):
        mine_ref = picks.at[SLOTS + k]
        b_send_to(k, 0, mine_ref, b_out.at[k, t], at_x(1))
        b_send_to(k, 1, mine_ref, b_out.at[k, t], at_x(-1))
        b_send_to(k, 2, mine_ref, b_out.at[k, t], sibling)
        copies["o", k] = pltpu.make_async_copy(mine_ref, b_out.at[k, t], own_sem.at[k])
        copies["o", k].start()

    lower, upper = pl.ds(0, half), pl.ds(half, half)

    def pass_second(k):
        low = b_out.at[k, t_of(-1)]
        b_arrived(k, 0, low)
        b_send_to(k, 3, b_out.at[k, t_of(-1), lower], b_out.at[k, t_of(-1), lower], at_x(1))
        b_send_to(k, 5, low, low, sibling)
        high = b_out.at[k, t_of(1)]
        b_arrived(k, 1, high)
        b_send_to(k, 4, b_out.at[k, t_of(1), upper], b_out.at[k, t_of(1), upper], at_x(-1))
        b_send_to(k, 6, high, high, sibling)

    def share_second(k):
        far_low = b_out.at[k, t_of(2), lower]
        b_arrived(k, 3, far_low)
        b_send_to(k, 7, far_low, far_low, sibling)
        far_up = b_out.at[k, t_of(2), upper]
        b_arrived(k, 4, far_up)
        b_send_to(k, 8, far_up, far_up, sibling)

    def close_second(k):
        b_arrived(k, 2, b_out.at[k, t_of(0, 1 - core)])
        b_arrived(k, 5, b_out.at[k, t_of(-1, 1 - core)])
        b_arrived(k, 6, b_out.at[k, t_of(1, 1 - core)])
        b_arrived(k, 7, b_out.at[k, t_of(2, 1 - core), lower])
        b_arrived(k, 8, b_out.at[k, t_of(2, 1 - core), upper])

    first_hop(0)
    first_hop(1)
    direct(0)
    for u in range(UNITS + 1):
        if u < UNITS:
            merged(u)
            if u + 2 < UNITS:
                first_hop(u + 2)
            if u + 1 < UNITS:
                direct(u + 1)
        if u >= 1:
            finish(u - 1)
            if u - 1 == SLOTS - 1:
                send_first()
            if u - 1 >= SLOTS:
                send_second(u - 1 - SLOTS)
            if u - 2 >= SLOTS:
                pass_second(u - 2 - SLOTS)
            if u - 3 >= SLOTS:
                share_second(u - 3 - SLOTS)
    pass_second(SLOTS - 1)
    share_second(SLOTS - 2)
    share_second(SLOTS - 1)
    for k in range(SLOTS):
        close_second(k)
        copies["o", k].wait()
    for d in range(1, NTM):
        come = (t + NTM - d) % NTM
        pltpu.make_async_remote_copy(
            src_ref=packed.at[0], dst_ref=p_out.at[come],
            send_sem=p_send.at[d], recv_sem=p_recv.at[d],
            device_id=sibling, device_id_type=MESH,
        ).wait_recv()
    copies["p", 0].wait()
    for copy in z_started:
        copy.wait_send()
    for u in range(UNITS):
        for s in (0, 1):
            for kind in ("a", "d", "m"):
                copies[kind, u, s].wait_send()
    for d in range(1, NTM):
        copies["p", d].wait_send()
    for k in range(SLOTS):
        for n in range(9):
            copies["b", k, n].wait_send()


def exchange(traces, owner, tiles):
    seg_count = traces.shape[0]
    rows = seg_count * BLOCK
    tab_hi, tab_lo = forward_table()
    vmem = pl.BlockSpec(memory_space=pltpu.VMEM)
    smem = pl.BlockSpec(memory_space=pltpu.SMEM)
    anywhere = pl.BlockSpec(memory_space=pl.ANY)
    half_units = (UNITS, 2, NG, 16, BLOCK)
    dma = pltpu.SemaphoreType.DMA
    return pl.pallas_call(
        exchange_kernel,
        out_shape=(
            jax.ShapeDtypeStruct((SLOTS, NTM, NG, 2, 16, BLOCK), BF),
            jax.ShapeDtypeStruct((NTM, 2 * NF, BLOCK), BF),
        ),
        in_specs=[vmem, vmem, vmem, smem, smem],
        out_specs=(anywhere, anywhere),
        scratch_shapes=[
            pltpu.VMEM((NZ, NG, 2, 16, BLOCK), BF),
            pltpu.VMEM((UNITS, NG, 2, 16, BLOCK), BF),
            pltpu.VMEM(half_units, BF),
            pltpu.VMEM(half_units, BF),
            pltpu.VMEM(half_units, BF),
            pltpu.VMEM(half_units, BF),
            pltpu.VMEM(half_units, BF),
            pltpu.VMEM(half_units, BF),
            pltpu.VMEM((NTM, 2 * NF, BLOCK), BF),
            pltpu.VMEM((NTM, UNITS * BLOCK, BLOCK), BF),
            pltpu.VMEM((NY, 8, 128), jnp.int32),
            pltpu.SMEM((NY, 8, 128), jnp.int32),
            dma((2, NZ // 2, CHUNKS)), dma((2, NZ // 2, CHUNKS)),
            dma((NY,)), dma((NY,)), dma((NY,)),
            dma((UNITS, 2)), dma((UNITS, 2)),
            dma((UNITS, 2)), dma((UNITS, 2)),
            dma((UNITS, 2)), dma((UNITS, 2)),
            dma((SLOTS, 9)), dma((SLOTS, 9)),
            dma((NTM,)), dma((NTM,)),
            dma((SLOTS + 1,)),
        ],
        compiler_params=pltpu.CompilerParams(
            collective_id=0, has_side_effects=True, vmem_limit_bytes=48 << 20
        ),
        name="exchange",
    )(traces.reshape(rows, NT), jnp.asarray(tab_hi), jnp.asarray(tab_lo), owner, tiles)


def stack_kernel(scale, counts, p_ref, b_ref, inv_hi, inv_lo, out, first, turned, high, low):
    k = pl.program_id(0)

    @pl.when(k == 0)
    def _():
        eye = (
            lax.broadcasted_iota(jnp.int32, (BLOCK, BLOCK), 0)
            == lax.broadcasted_iota(jnp.int32, (BLOCK, BLOCK), 1)
        )
        eye = jnp.where(eye, 1.0, 0.0).astype(BF)
        for g in range(NG):
            tile = p_ref[:, g * 16 : (g + 1) * 16, :]
            first[g] = nt_dot(eye, tile.reshape(BLOCK, BLOCK))
            wide = tile.astype(F32)
            wide = jnp.concatenate([-wide[:, 8:], wide[:, :8]], axis=1)
            turned[g] = nt_dot(eye, wide.astype(BF).reshape(BLOCK, BLOCK))

    shape = (8, BLOCK)
    mask = lax.broadcasted_iota(jnp.int32, shape, 1) % 8 == lax.broadcasted_iota(
        jnp.int32, shape, 0
    )
    mask = jnp.where(mask, 1.0, 0.0).astype(F32)[None]

    def group(g, carry):
        halves = []
        for s in (0, 1):
            rows = pl.ds(pl.multiple_of(k * 32 + s * 16, 16), 16)
            direct = first[g, rows, :][:, None, :] * mask
            crossed = turned[g, rows, :][:, None, :] * mask
            both = jnp.concatenate([direct, crossed], axis=1).astype(BF)
            halves.append(both.reshape(2 * NF, BLOCK))
        lhs = jnp.concatenate(halves, axis=1)
        rhs = jnp.concatenate([b_ref[t, g, s] for s in (0, 1) for t in range(NTM)], axis=0)
        cross = jnp.dot(lhs, rhs, preferred_element_type=F32).reshape(16, 16, BLOCK)
        rows = pl.ds(pl.multiple_of(g * 16, 16), 16)
        top = cross.astype(BF)
        high[:, rows, :] = top
        low[:, rows, :] = (cross - top.astype(F32)).astype(BF)
        return carry

    lax.fori_loop(0, NG, group, 0)
    factor = jnp.where(k < counts[0], scale, 0.0)
    for i in range(0, 16, 2):
        c_hi = jnp.concatenate([high[i], high[i + 1]], axis=1)
        c_lo = jnp.concatenate([low[i], low[i + 1]], axis=1)
        lagged = jnp.dot(inv_hi[...], c_hi, preferred_element_type=F32)
        lagged = lagged + jnp.dot(inv_lo[...], c_hi, preferred_element_type=F32)
        lagged = lagged + jnp.dot(inv_hi[...], c_lo, preferred_element_type=F32)
        out[:, i * BLOCK : (i + 2) * BLOCK] = lagged * factor


def stack(counts, p_all, b_all, scale):
    inv_hi, inv_lo = inverse_table()
    share = BLOCK // NTM
    return pl.pallas_call(
        functools.partial(stack_kernel, scale),
        grid=(SLOTS,),
        out_shape=jax.ShapeDtypeStruct((SLOTS, LAGS, share * BLOCK), F32),
        in_specs=[
            pl.BlockSpec(memory_space=pltpu.SMEM),
            pl.BlockSpec((NTM, 2 * NF, BLOCK), lambda k: (0, 0, 0)),
            pl.BlockSpec((None, NTM, NG, 2, 16, BLOCK), lambda k: (k, 0, 0, 0, 0, 0)),
            pl.BlockSpec((LAGS, 2 * NF), lambda k: (0, 0)),
            pl.BlockSpec((LAGS, 2 * NF), lambda k: (0, 0)),
        ],
        out_specs=pl.BlockSpec((None, LAGS, share * BLOCK), lambda k: (k, 0, 0)),
        scratch_shapes=[
            pltpu.VMEM((NG, BLOCK, BLOCK), F32),
            pltpu.VMEM((NG, BLOCK, BLOCK), F32),
            pltpu.VMEM((16, 2 * NF, BLOCK), BF),
            pltpu.VMEM((16, 2 * NF, BLOCK), BF),
        ],
        compiler_params=pltpu.CompilerParams(
            dimension_semantics=("arbitrary",), vmem_limit_bytes=32 << 20
        ),
        name="stack",
    )(counts, p_all, b_all, jnp.asarray(inv_hi), jnp.asarray(inv_lo))


def shards(traces, owner, tiles, counts):
    segments = traces.shape[0] * NTM
    b_all, p_all = exchange(traces, owner, tiles)
    return stack(counts, p_all, b_all, 1.0 / math.sqrt(segments * NF))


def solution(mesh):
    placed = (P("tm", "pair", None), P(), P("pair", None), P("pair"))
    return jax.shard_map(
        shards, mesh=mesh, in_specs=placed, out_specs=P("pair", None, "tm"), check_vma=False
    )
```

time: 260 us -> 103 us (0.40)
  waiting for transfers between devices: 175 us -> 0 us
  Pallas kernels: 0 us -> 96 us
  matrix products: 24.7 us -> 0 us
  local copies, waits for them, and re-layouts: 30.1 us -> 6.4 us
  between operations: 14.2 us -> 0.67 us
  starting transfers between devices: 12.6 us -> 0 us
  other arithmetic: 2.73 us -> 0 us
    all_gather x2 -> x0, waiting for transfers between devices: 168 us -> none  [the longest x1 154 us: shards(): every = lax.all_gather(white[None], 'pair', axis=0, tiled=True)]
    pallas_call x0 -> x2, Pallas kernels: none -> 96 us  [the longest x1 83.7 us: exchange(): pl.pallas_call(exchange_kernel, out_shape=(jax.ShapeDtypeStruct((SLOTS, N...]
    dot_general x7 -> x0, matrix products: 24.7 us -> none  [the longest x1 5.02 us: shards(): jnp.einsum('lf,qfx->qlx', cos_part, cross_real, precision=lax.Precision.H...]
    all_to_all x1 -> x0, starting transfers between devices: 12.6 us -> none  [shards(): lax.all_to_all(left, 'tm', split_axis=2, concat_axis=1, tiled=True)]
    all_to_all x1 -> x0, waiting for transfers between devices: 7.41 us -> none  [shards(): lax.all_to_all(left, 'tm', split_axis=2, concat_axis=1, tiled=True)]
    reshape x3 -> x0, local copies, waits for them, and re-layouts: 7.16 us -> none  [the longest x1 3.56 us: shards(): cross_real = cross_real.reshape(number, NF, share * block)]
    slice x3 -> x0, local copies, waits for them, and re-layouts: 4.08 us -> none  [the longest x1 3.95 us: shards(): right_imag = right_all[..., NF:]]
    gather x1 -> x0, local copies, waits for them, and re-layouts: 3.98 us -> none  [shards(): jnp.take(every, stored.reshape(-1), axis=0).reshape(slots, 2, rows, width)]
  transfers between devices with their start and end apart: 3 -> 0, of which waited for: 3 -> 0; matrix products, arithmetic and copies ran while one was open for 2% -> 0% of each run, Pallas kernels for 0% -> 0%
where the time goes in v1:
time: 103 us
  Pallas kernels  96 us (93%)
  local copies, waits for them, and re-layouts  6.4 us (6%)
    pallas_call x1, Pallas kernels, exchange(): pl.pallas_call(exchange_kernel, out_shape=(jax.ShapeDtypeStruct((SLOTS, N...  83.7 us
    pallas_call x1, Pallas kernels, stack(): pl.pallas_call(functools.partial(stack_kernel, scale), grid=(SLOTS,), out...  12.3 us
    unnamed x13, local copies, waits for them, and re-layouts  6.4 us

profile of v1, /device:TPU:1, one launch (start us, length us, event | category | flops | bytes accessed | tf_op | source)
XLA Modules:
  0.0 103.1 jit_solution(10025798282378577400)
XLA Ops:
  0.7 0.8 copy.9.tiles
  1.4 0.0 copy-start
  1.4 1.2 %copy-done = f32[2,128,1024]{2,1,0:T(8,128)S(1)} copy-done((f32[2,128,1024]{2,1,0:T(8,128)S(1)}, f32[2,128,1024]{2,1,0:T(8,128)}, u32[]{:S(2)}) %copy-start) | copy-done | bytes 1048600
  2.6 0.0 copy-start.1
  2.6 1.0 %copy-done.1 = bf16[256,1024]{1,0:T(8,128)(2,1)S(1)} copy-done((bf16[256,1024]{1,0:T(8,128)(2,1)S(1)}, bf16[256,1024]{1,0:T(8,128)(2,1)}, u32[]{:S(2)}) %copy-start.1) | copy-done | bytes 524312
  3.7 0.0 copy-start.2
  3.7 1.0 %copy-done.2 = bf16[256,1024]{1,0:T(8,128)(2,1)S(1)} copy-done((bf16[256,1024]{1,0:T(8,128)(2,1)S(1)}, bf16[256,1024]{1,0:T(8,128)(2,1)}, u32[]{:S(2)}) %copy-start.2) | copy-done | bytes 524312
  4.7 0.0 copy-start.5
  4.7 0.7 copy-done.5
  5.4 83.7 %exchange.1 = (bf16[3,8,16,2,16,128]{5,4,3,2,1,0:T(8,128)(2,1)S(1)}, bf16[8,256,128]{2,1,0:T(8,128)(2,1)S(1)}) custom-call(f32[256,1024]{1,0:T(8,128)S(1)} %bitcast.1, bf16[256,1024]{1,0:T(8,128)(2,1)S(1)} %copy-done.2, bf16[256,1024]{1,0:T(8,128)(2,1)S(1)} %copy-done.1, s32[64]{0:T(128)S(1)} %copy-done.5, s32[3,2]{1,0:T(4,128)S(1)} %copy.9.tiles), custom_call_target="tpu_custom_call" | custom-call | tf_op jit(solution)/shard_map/exchange/pallas_call | solution.py:368
  89.1 0.0 copy-start.3
  89.1 0.8 copy-done.3
  89.9 0.0 copy-start.4
  89.9 0.8 copy-done.4
  90.8 12.3 %stack.1 = f32[3,128,2048]{2,1,0:T(8,128)} custom-call(s32[1]{0:T(128)S(6)} %copy.10.counts, bf16[8,256,128]{2,1,0:T(8,128)(2,1)S(1)} %get-tuple-element.7.p_ref, bf16[3,8,16,2,16,128]{5,4,3,2,1,0:T(8,128)(2,1)S(1)} %get-tuple-element.8.b_ref, bf16[128,256]{1,0:T(8,128)(2,1)S(1)} %copy-done.4, bf16[128,256]{1,0:T(8,128)(2,1)S(1)} %copy-done.3), custom_call_target="tpu_custom_call" | custom-call | tf_op jit(solution)/shard_map/stack/pallas_call | solution.py:459
Async XLA Ops:
  1.4 1.2 %copy-start = (f32[2,128,1024]{2,1,0:T(8,128)S(1)}, f32[2,128,1024]{2,1,0:T(8,128)}, u32[]{:S(2)}) copy-start(f32[2,128,1024]{2,1,0:T(8,128)} %param.8) | copy-start | bytes 3145732
  2.6 1.0 %copy-start.1 = (bf16[256,1024]{1,0:T(8,128)(2,1)S(1)}, bf16[256,1024]{1,0:T(8,128)(2,1)}, u32[]{:S(2)}) copy-start(bf16[256,1024]{1,0:T(8,128)(2,1)} %constant.9.clone.tab_lo) | copy-start | bytes 1572868
  3.7 1.0 %copy-start.2 = (bf16[256,1024]{1,0:T(8,128)(2,1)S(1)}, bf16[256,1024]{1,0:T(8,128)(2,1)}, u32[]{:S(2)}) copy-start(bf16[256,1024]{1,0:T(8,128)(2,1)} %constant.8.clone.tab_hi) | copy-start | bytes 1572868
  4.7 0.7 copy-start.5
  89.1 0.8 copy-start.3
  89.9 0.8 copy-start.4

commit v2 on v1

--- a/solution.py
+++ b/solution.py
@@ -51,13 +51,17 @@
     return split(parts.reshape(LAGS, 2 * NF))
 
 
+def in_hbm(array):
+    return pltpu.with_memory_space_constraint(jnp.asarray(array), pltpu.HBM)
+
+
 def nt_dot(a, b):
     return lax.dot_general(a, b, (((1,), (1,)), ((), ())), preferred_element_type=F32)
 
 
 def exchange_kernel(
-    traces, tab_hi, tab_lo, owner, tiles, b_out, p_out,
-    slabs, picks, stage_a, stage_d, stage_m, got_x, got_p, got_m,
+    traces_hbm, hi_hbm, lo_hbm, owner_hbm, tiles_hbm, b_out, p_out,
+    owner, tiles, traces, tab_hi, tab_lo, load_sem, slabs, picks, stage_a, stage_d, stage_m, got_x, got_p, got_m,
     packed, choose, req_v, req_s,
     z_send, z_recv, r_send, r_recv, r_loc, a_send, a_recv, d_send, d_recv, m_send, m_recv,
     b_send, b_recv, p_send, p_recv, own_sem,
@@ -85,6 +89,20 @@
     greet = [at_z(1), at_z(-1)] + [at_y(d) for d in (1, 2, 3)] + [at_t(d) for d in range(1, NTM)]
     for who in greet:
         pl.semaphore_signal(barrier, inc=1, device_id=who, device_id_type=MESH)
+
+    loads = [
+        pltpu.make_async_copy(src, dst, load_sem.at[n])
+        for n, (src, dst) in enumerate(
+            (
+                (hi_hbm, tab_hi), (traces_hbm, traces), (lo_hbm, tab_lo),
+                (owner_hbm, owner), (tiles_hbm, tiles),
+            )
+        )
+    ]
+    for load in loads:
+        load.start()
+    for load in loads:
+        load.wait()
 
     values = traces[...]
     v_hi = values.astype(BF)
@@ -114,7 +132,7 @@
     lane = lax.broadcasted_iota(jnp.int32, (8, 128), 1)
     row = jnp.zeros((8, 128), jnp.int32)
     for u in range(UNITS):
-        wanted = owner[tiles[u % SLOTS, u // SLOTS]]
+        wanted = owner[tiles[u // SLOTS, u % SLOTS]]
         mine.append(wanted)
         row = jnp.where(lane == u, wanted, row)
     req_v[0] = row
@@ -165,20 +183,25 @@
         copy.start()
         r_copies.append(copy)
 
-    r_i = lax.broadcasted_iota(jnp.int32, (BLOCK, BLOCK), 0)
-    c_i = lax.broadcasted_iota(jnp.int32, (BLOCK, BLOCK), 1)
-    for to in range(NTM):
+    def build_choose(to):
+        r_i = lax.broadcasted_iota(jnp.int32, (BLOCK, BLOCK), 0)
+        c_i = lax.broadcasted_iota(jnp.int32, (BLOCK, BLOCK), 1)
         inside = (r_i >= 16 * to) & (r_i < 16 * to + 16)
+        lanes = slice(to % 2 * BLOCK, to % 2 * BLOCK + BLOCK)
         for part in range(UNITS):
             hit = inside & (c_i - r_i == 16 * part - 16 * to)
-            choose[to, pl.ds(part * BLOCK, BLOCK), :] = jnp.where(hit, 1.0, 0.0).astype(BF)
-
-    for copy in r_copies:
-        copy.wait()
-    for d in (1, 2, 3):
-        local = pltpu.make_async_copy(req_v.at[d], req_s.at[d], r_loc.at[d])
-        local.start()
-        local.wait()
+            choose[to // 2, pl.ds(part * BLOCK, BLOCK), lanes] = jnp.where(hit, 1.0, 0.0).astype(BF)
+
+    def fetch_requests():
+        for copy in r_copies:
+            copy.wait()
+        local = [
+            pltpu.make_async_copy(req_v.at[d], req_s.at[d], r_loc.at[d]) for d in (1, 2, 3)
+        ]
+        for copy in local:
+            copy.start()
+        for copy in local:
+            copy.wait()
 
     for step in range(1, last + 1):
         for way, c in z_pieces(step):
@@ -186,6 +209,11 @@
             copy = z_copy(way, step, c)
             copy.start()
             z_started.append(copy)
+        build_choose(step)
+        if step == 1:
+            build_choose(0)
+        if step == 4:
+            fetch_requests()
         if step == last:
             for c in range(CHUNKS):
                 for way in (0, 1):
@@ -246,12 +274,16 @@
         second = jnp.where(column == down, got_p[u, 1], got_m[u, 1])
         picks[u, :, 1] = jnp.where(own, slabs[index, :, 1], second)
 
-    def send_first():
+    def send_first(pairs):
         lanes = jnp.concatenate(
             [picks[u, :, s].reshape(2 * NF, BLOCK) for u in range(SLOTS) for s in (0, 1)], axis=1
         )
-        for to in range(NTM):
-            packed[to] = jnp.dot(lanes, choose[to], preferred_element_type=F32).astype(BF)
+        for two in pairs:
+            both = jnp.dot(lanes, choose[two], preferred_element_type=F32).astype(BF)
+            packed[2 * two] = both[:, :BLOCK]
+            packed[2 * two + 1] = both[:, BLOCK:]
+
+    def start_first():
         for d in range(1, NTM):
             to = (t + d) % NTM
             copies["p", d] = send(
@@ -322,7 +354,10 @@
         if u >= 1:
             finish(u - 1)
             if u - 1 == SLOTS - 1:
-                send_first()
+                send_first((0, 1))
+            if u - 1 == SLOTS:
+                send_first((2, 3))
+                start_first()
             if u - 1 >= SLOTS:
                 send_second(u - 1 - SLOTS)
             if u - 2 >= SLOTS:
@@ -360,8 +395,7 @@
     seg_count = traces.shape[0]
     rows = seg_count * BLOCK
     tab_hi, tab_lo = forward_table()
-    vmem = pl.BlockSpec(memory_space=pltpu.VMEM)
-    smem = pl.BlockSpec(memory_space=pltpu.SMEM)
+    hbm = pl.BlockSpec(memory_space=pltpu.HBM)
     anywhere = pl.BlockSpec(memory_space=pl.ANY)
     half_units = (UNITS, 2, NG, 16, BLOCK)
     dma = pltpu.SemaphoreType.DMA
@@ -371,9 +405,15 @@
             jax.ShapeDtypeStruct((SLOTS, NTM, NG, 2, 16, BLOCK), BF),
             jax.ShapeDtypeStruct((NTM, 2 * NF, BLOCK), BF),
         ),
-        in_specs=[vmem, vmem, vmem, smem, smem],
+        in_specs=[hbm, hbm, hbm, hbm, hbm],
         out_specs=(anywhere, anywhere),
         scratch_shapes=[
+            pltpu.SMEM(owner.shape, jnp.int32),
+            pltpu.SMEM(tiles.shape[::-1], jnp.int32),
+            pltpu.VMEM((rows, NT), F32),
+            pltpu.VMEM((2 * NF, NT), BF),
+            pltpu.VMEM((2 * NF, NT), BF),
+            dma((5,)),
             pltpu.VMEM((NZ, NG, 2, 16, BLOCK), BF),
             pltpu.VMEM((UNITS, NG, 2, 16, BLOCK), BF),
             pltpu.VMEM(half_units, BF),
@@ -383,7 +423,7 @@
             pltpu.VMEM(half_units, BF),
             pltpu.VMEM(half_units, BF),
             pltpu.VMEM((NTM, 2 * NF, BLOCK), BF),
-            pltpu.VMEM((NTM, UNITS * BLOCK, BLOCK), BF),
+            pltpu.VMEM((NTM // 2, UNITS * BLOCK, 2 * BLOCK), BF),
             pltpu.VMEM((NY, 8, 128), jnp.int32),
             pltpu.SMEM((NY, 8, 128), jnp.int32),
             dma((2, NZ // 2, CHUNKS)), dma((2, NZ // 2, CHUNKS)),
@@ -399,7 +439,7 @@
             collective_id=0, has_side_effects=True, vmem_limit_bytes=48 << 20
         ),
         name="exchange",
-    )(traces.reshape(rows, NT), jnp.asarray(tab_hi), jnp.asarray(tab_lo), owner, tiles)
+    )(*[in_hbm(a) for a in (traces.reshape(rows, NT), tab_hi, tab_lo, owner, tiles.T)])
 
 
 def stack_kernel(scale, counts, p_ref, b_ref, inv_hi, inv_lo, out, first, turned, high, low):
@@ -425,7 +465,7 @@
     )
     mask = jnp.where(mask, 1.0, 0.0).astype(F32)[None]
 
-    def group(g, carry):
+    def group(g):
         halves = []
         for s in (0, 1):
             rows = pl.ds(pl.multiple_of(k * 32 + s * 16, 16), 16)
@@ -436,13 +476,13 @@
         lhs = jnp.concatenate(halves, axis=1)
         rhs = jnp.concatenate([b_ref[t, g, s] for s in (0, 1) for t in range(NTM)], axis=0)
         cross = jnp.dot(lhs, rhs, preferred_element_type=F32).reshape(16, 16, BLOCK)
-        rows = pl.ds(pl.multiple_of(g * 16, 16), 16)
+        rows = slice(g * 16, g * 16 + 16)
         top = cross.astype(BF)
         high[:, rows, :] = top
         low[:, rows, :] = (cross - top.astype(F32)).astype(BF)
-        return carry
-
-    lax.fori_loop(0, NG, group, 0)
+
+    for g in range(NG):
+        group(g)
     factor = jnp.where(k < counts[0], scale, 0.0)
     for i in range(0, 16, 2):
         c_hi = jnp.concatenate([high[i], high[i + 1]], axis=1)
@@ -478,7 +518,7 @@
             dimension_semantics=("arbitrary",), vmem_limit_bytes=32 << 20
         ),
         name="stack",
-    )(counts, p_all, b_all, jnp.asarray(inv_hi), jnp.asarray(inv_lo))
+    )(counts, p_all, b_all, in_hbm(inv_hi), in_hbm(inv_lo))
 
 
 def shards(traces, owner, tiles, counts):

time: 103 us -> 91.2 us (0.89)
  local copies, waits for them, and re-layouts: 6.4 us -> 0 us
  Pallas kernels: 96 us -> 90.3 us
    unnamed x13 -> x0, local copies, waits for them, and re-layouts: 6.4 us -> none
    pallas_call x1, Pallas kernels: 12.3 us -> 7.03 us  [stack(): pl.pallas_call(functools.partial(stack_kernel, scale), grid=(SLOTS,), out...]
where the time goes in v2:
time: 91.2 us; the launch traced here: 91 us
  Pallas kernels  90.3 us (99%)
    pallas_call x1, Pallas kernels, exchange(): pl.pallas_call(exchange_kernel, out_shape=(jax.ShapeDtypeStruct((SLOTS, N...  83.3 us
    pallas_call x1, Pallas kernels, stack(): pl.pallas_call(functools.partial(stack_kernel, scale), grid=(SLOTS,), out...  7.03 us

profile of v2, /device:TPU:1, one launch (start us, length us, event | category | flops | bytes accessed | tf_op | source)
XLA Modules:
  0.0 91.0 jit_solution(8786215465213079816)
XLA Ops:
  0.7 83.3 %exchange.1 = (bf16[3,8,16,2,16,128]{5,4,3,2,1,0:T(8,128)(2,1)S(1)}, bf16[8,256,128]{2,1,0:T(8,128)(2,1)S(1)}) custom-call(f32[256,1024]{1,0:T(8,128)} %bitcast.2, bf16[256,1024]{1,0:T(8,128)(2,1)} %constant.8.clone.hi_hbm, bf16[256,1024]{1,0:T(8,128)(2,1)} %constant.9.clone.lo_hbm, s32[64]{0:T(128)} %owner_hbm.1, s32[2,3]{1,0:T(2,128)} %bitcast.3), custom_call_target="tpu_custom_call" | custom-call | tf_op jit(solution)/shard_map/exchange/pallas_call | solution.py:402
  84.0 7.0 %stack.1 = f32[3,128,2048]{2,1,0:T(8,128)} custom-call(s32[1]{0:T(128)S(6)} %copy.9.counts, bf16[8,256,128]{2,1,0:T(8,128)(2,1)S(1)} %get-tuple-element.7.p_ref, bf16[3,8,16,2,16,128]{5,4,3,2,1,0:T(8,128)(2,1)S(1)} %get-tuple-element.8.b_ref, bf16[128,256]{1,0:T(8,128)(2,1)} %constant.10.clone.inv_hi, bf16[128,256]{1,0:T(8,128)(2,1)} %constant.11.clone.inv_lo), custom_call_target="tpu_custom_call" | custom-call | tf_op jit(solution)/shard_map/stack/pallas_call | solution.py:499

commit v3 on v2

--- a/solution.py
+++ b/solution.py
@@ -59,10 +59,15 @@
     return lax.dot_general(a, b, (((1,), (1,)), ((), ())), preferred_element_type=F32)
 
 
+def identity(size):
+    row = lax.broadcasted_iota(jnp.int32, (size, size), 0)
+    return jnp.where(row == lax.broadcasted_iota(jnp.int32, (size, size), 1), 1.0, 0.0).astype(BF)
+
+
 def exchange_kernel(
     traces_hbm, hi_hbm, lo_hbm, owner_hbm, tiles_hbm, b_out, p_out,
     owner, tiles, traces, tab_hi, tab_lo, load_sem, slabs, picks, stage_a, stage_d, stage_m, got_x, got_p, got_m,
-    packed, choose, req_v, req_s,
+    packed, req_v, req_s,
     z_send, z_recv, r_send, r_recv, r_loc, a_send, a_recv, d_send, d_recv, m_send, m_recv,
     b_send, b_recv, p_send, p_recv, own_sem,
 ):
@@ -132,7 +137,7 @@
     lane = lax.broadcasted_iota(jnp.int32, (8, 128), 1)
     row = jnp.zeros((8, 128), jnp.int32)
     for u in range(UNITS):
-        wanted = owner[tiles[u // SLOTS, u % SLOTS]]
+        wanted = owner[tiles[1 - u % 2, u // 2]]
         mine.append(wanted)
         row = jnp.where(lane == u, wanted, row)
     req_v[0] = row
@@ -182,15 +187,6 @@
         )
         copy.start()
         r_copies.append(copy)
-
-    def build_choose(to):
-        r_i = lax.broadcasted_iota(jnp.int32, (BLOCK, BLOCK), 0)
-        c_i = lax.broadcasted_iota(jnp.int32, (BLOCK, BLOCK), 1)
-        inside = (r_i >= 16 * to) & (r_i < 16 * to + 16)
-        lanes = slice(to % 2 * BLOCK, to % 2 * BLOCK + BLOCK)
-        for part in range(UNITS):
-            hit = inside & (c_i - r_i == 16 * part - 16 * to)
-            choose[to // 2, pl.ds(part * BLOCK, BLOCK), lanes] = jnp.where(hit, 1.0, 0.0).astype(BF)
 
     def fetch_requests():
         for copy in r_copies:
@@ -209,9 +205,6 @@
             copy = z_copy(way, step, c)
             copy.start()
             z_started.append(copy)
-        build_choose(step)
-        if step == 1:
-            build_choose(0)
         if step == 4:
             fetch_requests()
         if step == last:
@@ -235,6 +228,7 @@
         return copy
 
     copies = {}
+    eye = identity(BLOCK)
 
     def first_hop(u):
         index, _ = asked(2, u)
@@ -269,28 +263,25 @@
             copies["m", u, s].wait_recv()
         up, down = (y + 1) % NY, (y + NY - 1) % NY
         own = column == y
-        first = jnp.where(column == up, got_m[u, 0], got_p[u, 0])
-        picks[u, :, 0] = jnp.where(own, slabs[index, :, 0], first)
-        second = jnp.where(column == down, got_p[u, 1], got_m[u, 1])
-        picks[u, :, 1] = jnp.where(own, slabs[index, :, 1], second)
-
-    def send_first(pairs):
-        lanes = jnp.concatenate(
-            [picks[u, :, s].reshape(2 * NF, BLOCK) for u in range(SLOTS) for s in (0, 1)], axis=1
-        )
-        for two in pairs:
-            both = jnp.dot(lanes, choose[two], preferred_element_type=F32).astype(BF)
-            packed[2 * two] = both[:, :BLOCK]
-            packed[2 * two + 1] = both[:, BLOCK:]
-
-    def start_first():
+        low = jnp.where(column == up, got_m[u, 0], got_p[u, 0])
+        low = jnp.where(own, slabs[index, :, 0], low)
+        high = jnp.where(column == down, got_p[u, 1], got_m[u, 1])
+        high = jnp.where(own, slabs[index, :, 1], high)
+        return low, high
+
+    def send_first(k, value):
+        for seg in (0, 1):
+            turned = nt_dot(eye, value[seg].reshape(2 * NF, BLOCK)).astype(BF)
+            packed[k, :, seg] = turned.reshape(NTM, 16, 2 * NF)
         for d in range(1, NTM):
             to = (t + d) % NTM
-            copies["p", d] = send(
-                packed.at[to], p_out.at[t], p_send.at[d], p_recv.at[d], at_t(d)
+            copies["p", k, d] = send(
+                packed.at[k, to], p_out.at[t, k], p_send.at[k, d], p_recv.at[k, d], at_t(d)
             )
-        copies["p", 0] = pltpu.make_async_copy(packed.at[t], p_out.at[t], own_sem.at[SLOTS])
-        copies["p", 0].start()
+        copies["p", k, 0] = pltpu.make_async_copy(
+            packed.at[k, t], p_out.at[t, k], own_sem.at[SLOTS + k]
+        )
+        copies["p", k, 0].start()
 
     half = NG // 2
 
@@ -306,8 +297,9 @@
             device_id=sibling, device_id_type=MESH,
         ).wait_recv()
 
-    def send_second(k):
-        mine_ref = picks.at[SLOTS + k]
+    def send_second(k, value):
+        picks[k, :, 0], picks[k, :, 1] = value
+        mine_ref = picks.at[k]
         b_send_to(k, 0, mine_ref, b_out.at[k, t], at_x(1))
         b_send_to(k, 1, mine_ref, b_out.at[k, t], at_x(-1))
         b_send_to(k, 2, mine_ref, b_out.at[k, t], sibling)
@@ -351,42 +343,39 @@
                 first_hop(u + 2)
             if u + 1 < UNITS:
                 direct(u + 1)
-        if u >= 1:
-            finish(u - 1)
-            if u - 1 == SLOTS - 1:
-                send_first((0, 1))
-            if u - 1 == SLOTS:
-                send_first((2, 3))
-                start_first()
-            if u - 1 >= SLOTS:
-                send_second(u - 1 - SLOTS)
-            if u - 2 >= SLOTS:
-                pass_second(u - 2 - SLOTS)
-            if u - 3 >= SLOTS:
-                share_second(u - 3 - SLOTS)
-    pass_second(SLOTS - 1)
-    share_second(SLOTS - 2)
+        if u == 0:
+            continue
+        k, role = (u - 1) // 2, (u - 1) % 2
+        value = finish(u - 1)
+        if role == 0:
+            send_second(k, value)
+            if k > 0:
+                share_second(k - 1)
+        else:
+            send_first(k, value)
+            pass_second(k)
     share_second(SLOTS - 1)
     for k in range(SLOTS):
         close_second(k)
         copies["o", k].wait()
-    for d in range(1, NTM):
-        come = (t + NTM - d) % NTM
-        pltpu.make_async_remote_copy(
-            src_ref=packed.at[0], dst_ref=p_out.at[come],
-            send_sem=p_send.at[d], recv_sem=p_recv.at[d],
-            device_id=sibling, device_id_type=MESH,
-        ).wait_recv()
-    copies["p", 0].wait()
+    for k in range(SLOTS):
+        for d in range(1, NTM):
+            come = (t + NTM - d) % NTM
+            pltpu.make_async_remote_copy(
+                src_ref=packed.at[k, 0], dst_ref=p_out.at[come, k],
+                send_sem=p_send.at[k, d], recv_sem=p_recv.at[k, d],
+                device_id=sibling, device_id_type=MESH,
+            ).wait_recv()
+        copies["p", k, 0].wait()
     for copy in z_started:
         copy.wait_send()
     for u in range(UNITS):
         for s in (0, 1):
             for kind in ("a", "d", "m"):
                 copies[kind, u, s].wait_send()
-    for d in range(1, NTM):
-        copies["p", d].wait_send()
     for k in range(SLOTS):
+        for d in range(1, NTM):
+            copies["p", k, d].wait_send()
         for n in range(9):
             copies["b", k, n].wait_send()
 
@@ -403,7 +392,7 @@
         exchange_kernel,
         out_shape=(
             jax.ShapeDtypeStruct((SLOTS, NTM, NG, 2, 16, BLOCK), BF),
-            jax.ShapeDtypeStruct((NTM, 2 * NF, BLOCK), BF),
+            jax.ShapeDtypeStruct((NTM, SLOTS, 2, 16, 2 * NF), BF),
         ),
         in_specs=[hbm, hbm, hbm, hbm, hbm],
         out_specs=(anywhere, anywhere),
@@ -415,15 +404,14 @@
             pltpu.VMEM((2 * NF, NT), BF),
             dma((5,)),
             pltpu.VMEM((NZ, NG, 2, 16, BLOCK), BF),
-            pltpu.VMEM((UNITS, NG, 2, 16, BLOCK), BF),
+            pltpu.VMEM((SLOTS, NG, 2, 16, BLOCK), BF),
             pltpu.VMEM(half_units, BF),
             pltpu.VMEM(half_units, BF),
             pltpu.VMEM(half_units, BF),
             pltpu.VMEM(half_units, BF),
             pltpu.VMEM(half_units, BF),
             pltpu.VMEM(half_units, BF),
-            pltpu.VMEM((NTM, 2 * NF, BLOCK), BF),
-            pltpu.VMEM((NTM // 2, UNITS * BLOCK, 2 * BLOCK), BF),
+            pltpu.VMEM((SLOTS, NTM, 2, 16, 2 * NF), BF),
             pltpu.VMEM((NY, 8, 128), jnp.int32),
             pltpu.SMEM((NY, 8, 128), jnp.int32),
             dma((2, NZ // 2, CHUNKS)), dma((2, NZ // 2, CHUNKS)),
@@ -432,8 +420,8 @@
             dma((UNITS, 2)), dma((UNITS, 2)),
             dma((UNITS, 2)), dma((UNITS, 2)),
             dma((SLOTS, 9)), dma((SLOTS, 9)),
-            dma((NTM,)), dma((NTM,)),
-            dma((SLOTS + 1,)),
+            dma((SLOTS, NTM)), dma((SLOTS, NTM)),
+            dma((2 * SLOTS,)),
         ],
         compiler_params=pltpu.CompilerParams(
             collective_id=0, has_side_effects=True, vmem_limit_bytes=48 << 20
@@ -442,18 +430,20 @@
     )(*[in_hbm(a) for a in (traces.reshape(rows, NT), tab_hi, tab_lo, owner, tiles.T)])
 
 
-def stack_kernel(scale, counts, p_ref, b_ref, inv_hi, inv_lo, out, first, turned, high, low):
+def stack_kernel(scale, counts, p_ref, b_ref, inv_hi, inv_lo, out, natural, first, turned, high, low):
     k = pl.program_id(0)
 
     @pl.when(k == 0)
     def _():
-        eye = (
-            lax.broadcasted_iota(jnp.int32, (BLOCK, BLOCK), 0)
-            == lax.broadcasted_iota(jnp.int32, (BLOCK, BLOCK), 1)
-        )
-        eye = jnp.where(eye, 1.0, 0.0).astype(BF)
+        eye = identity(2 * NF)
+        used = SLOTS * 32
+        pad = jnp.zeros((2 * NF, BLOCK - used), BF)
+        for t in range(NTM):
+            back = nt_dot(eye, p_ref[t].reshape(used, 2 * NF)).astype(BF)
+            natural[t] = jnp.concatenate([back, pad], axis=1)
+        eye = identity(BLOCK)
         for g in range(NG):
-            tile = p_ref[:, g * 16 : (g + 1) * 16, :]
+            tile = natural[:, g * 16 : (g + 1) * 16, :]
             first[g] = nt_dot(eye, tile.reshape(BLOCK, BLOCK))
             wide = tile.astype(F32)
             wide = jnp.concatenate([-wide[:, 8:], wide[:, :8]], axis=1)
@@ -502,13 +492,14 @@
         out_shape=jax.ShapeDtypeStruct((SLOTS, LAGS, share * BLOCK), F32),
         in_specs=[
             pl.BlockSpec(memory_space=pltpu.SMEM),
-            pl.BlockSpec((NTM, 2 * NF, BLOCK), lambda k: (0, 0, 0)),
+            pl.BlockSpec((NTM, SLOTS, 2, 16, 2 * NF), lambda k: (0, 0, 0, 0, 0)),
             pl.BlockSpec((None, NTM, NG, 2, 16, BLOCK), lambda k: (k, 0, 0, 0, 0, 0)),
             pl.BlockSpec((LAGS, 2 * NF), lambda k: (0, 0)),
             pl.BlockSpec((LAGS, 2 * NF), lambda k: (0, 0)),
         ],
         out_specs=pl.BlockSpec((None, LAGS, share * BLOCK), lambda k: (k, 0, 0)),
         scratch_shapes=[
+            pltpu.VMEM((NTM, 2 * NF, BLOCK), BF),
             pltpu.VMEM((NG, BLOCK, BLOCK), F32),
             pltpu.VMEM((NG, BLOCK, BLOCK), F32),
             pltpu.VMEM((16, 2 * NF, BLOCK), BF),

time: 91.2 us -> 87.2 us (0.956)
  Pallas kernels: 90.3 us -> 86.4 us
    pallas_call x1, Pallas kernels: 83.3 us -> 79 us  [exchange(): pl.pallas_call(exchange_kernel, out_shape=(jax.ShapeDtypeStruct((SLOTS, N...]
where the time goes in v3:
time: 87.2 us; the launch traced here: 87 us
  Pallas kernels  86.4 us (99%)
    pallas_call x1, Pallas kernels, exchange(): pl.pallas_call(exchange_kernel, out_shape=(jax.ShapeDtypeStruct((SLOTS, N...  79 us
    pallas_call x1, Pallas kernels, stack(): pl.pallas_call(functools.partial(stack_kernel, scale), grid=(SLOTS,), out...  7.36 us

profile of v3, /device:TPU:1, one launch (start us, length us, event | category | flops | bytes accessed | tf_op | source)
XLA Modules:
  0.0 87.0 jit_solution(7791126984508623119)
XLA Ops:
  0.7 79.0 %exchange.1 = (bf16[3,8,16,2,16,128]{5,4,3,2,1,0:T(8,128)(2,1)S(1)}, bf16[8,3,2,16,256]{4,3,2,1,0:T(8,128)(2,1)S(1)}) custom-call(f32[256,1024]{1,0:T(8,128)} %bitcast.2, bf16[256,1024]{1,0:T(8,128)(2,1)} %constant.8.clone.hi_hbm, bf16[256,1024]{1,0:T(8,128)(2,1)} %constant.9.clone.lo_hbm, s32[64]{0:T(128)} %owner_hbm.1, s32[2,3]{1,0:T(2,128)} %bitcast.3), custom_call_target="tpu_custom_call" | custom-call | tf_op jit(solution)/shard_map/exchange/pallas_call | solution.py:391
  79.7 7.4 %stack.1 = f32[3,128,2048]{2,1,0:T(8,128)} custom-call(s32[1]{0:T(128)S(6)} %copy.9.counts, bf16[8,3,2,16,256]{4,3,2,1,0:T(8,128)(2,1)S(1)} %get-tuple-element.7.p_ref, bf16[3,8,16,2,16,128]{5,4,3,2,1,0:T(8,128)(2,1)S(1)} %get-tuple-element.8.b_ref, bf16[128,256]{1,0:T(8,128)(2,1)} %constant.10.clone.inv_hi, bf16[128,256]{1,0:T(8,128)(2,1)} %constant.11.clone.inv_lo), custom_call_target="tpu_custom_call" | custom-call | tf_op jit(solution)/shard_map/stack/pallas_call | solution.py:489

commit v4 on v3

--- a/solution.py
+++ b/solution.py
@@ -23,7 +23,7 @@
 SLOTS = 3
 UNITS = 2 * SLOTS
 CHUNKS = 4
-GC = NG // CHUNKS
+GC = 2 * NG // CHUNKS
 BF = jnp.bfloat16
 F32 = jnp.float32
 MESH = pl.DeviceIdType.MESH
@@ -95,49 +95,50 @@
     for who in greet:
         pl.semaphore_signal(barrier, inc=1, device_id=who, device_id_type=MESH)
 
-    loads = [
-        pltpu.make_async_copy(src, dst, load_sem.at[n])
-        for n, (src, dst) in enumerate(
-            (
-                (hi_hbm, tab_hi), (traces_hbm, traces), (lo_hbm, tab_lo),
-                (owner_hbm, owner), (tiles_hbm, tiles),
-            )
-        )
+    def load(n, src, dst):
+        copy = pltpu.make_async_copy(src, dst, load_sem.at[n])
+        copy.start()
+        return copy
+
+    rows = [pl.ds(seg * BLOCK, BLOCK) for seg in (0, 1)]
+    early = [
+        load(0, owner_hbm, owner), load(1, tiles_hbm, tiles),
+        load(2, traces_hbm.at[rows[0]], traces.at[rows[0]]),
+        load(3, hi_hbm, tab_hi), load(4, lo_hbm, tab_lo),
     ]
-    for load in loads:
-        load.start()
-    for load in loads:
-        load.wait()
-
-    values = traces[...]
-    v_hi = values.astype(BF)
-    v_lo = (values - v_hi.astype(F32)).astype(BF)
-    spec = nt_dot(tab_hi[...], v_hi) + (nt_dot(tab_hi[...], v_lo) + nt_dot(tab_lo[...], v_hi))
-    real, imag = spec[:NF], spec[NF:]
-    power = real * real + imag * imag
-    width = power.shape[1]
-    bin_of = lax.broadcasted_iota(jnp.int32, power.shape, 0)
-    total = power
-    for step in (1, 2):
-        ahead = pltpu.roll(power, NF - step, 0)
-        behind = pltpu.roll(power, step, 0)
-        total = total + jnp.where(bin_of < NF - step, ahead, 0.0)
-        total = total + jnp.where(bin_of >= step, behind, 0.0)
-    edge = jnp.minimum(jnp.minimum(bin_of, NF - 1 - bin_of), 2)
-    smooth = total / (edge + 3).astype(F32)
-    level = jnp.sum(power, axis=0, keepdims=True) * (1.0 / NF)
-    factor = lax.rsqrt(smooth + 0.05 * level + 1e-06)
-    white = jnp.concatenate(
-        [(real * factor).reshape(NG, 8, width), (imag * factor).reshape(NG, 8, width)], axis=1
-    ).astype(BF)
-    slabs[z, :, 0] = white[:, :, :BLOCK]
-    slabs[z, :, 1] = white[:, :, BLOCK:]
+    late = load(5, traces_hbm.at[rows[1]], traces.at[rows[1]])
+    for copy in early:
+        copy.wait()
+
+    def transform(seg):
+        values = traces[rows[seg], :]
+        v_hi = values.astype(BF)
+        v_lo = (values - v_hi.astype(F32)).astype(BF)
+        spec = nt_dot(tab_hi[...], v_hi) + (nt_dot(tab_hi[...], v_lo) + nt_dot(tab_lo[...], v_hi))
+        real, imag = spec[:NF], spec[NF:]
+        power = real * real + imag * imag
+        bin_of = lax.broadcasted_iota(jnp.int32, power.shape, 0)
+        total = power
+        for step in (1, 2):
+            ahead = pltpu.roll(power, NF - step, 0)
+            behind = pltpu.roll(power, step, 0)
+            total = total + jnp.where(bin_of < NF - step, ahead, 0.0)
+            total = total + jnp.where(bin_of >= step, behind, 0.0)
+        edge = jnp.minimum(jnp.minimum(bin_of, NF - 1 - bin_of), 2)
+        smooth = total / (edge + 3).astype(F32)
+        level = jnp.sum(power, axis=0, keepdims=True) * (1.0 / NF)
+        factor = lax.rsqrt(smooth + 0.05 * level + 1e-06)
+        slabs[z, seg] = jnp.concatenate(
+            [(real * factor).reshape(NG, 8, BLOCK), (imag * factor).reshape(NG, 8, BLOCK)], axis=1
+        ).astype(BF)
+
+    transform(0)
 
     mine = []
     lane = lax.broadcasted_iota(jnp.int32, (8, 128), 1)
     row = jnp.zeros((8, 128), jnp.int32)
     for u in range(UNITS):
-        wanted = owner[tiles[1 - u % 2, u // 2]]
+        wanted = owner[tiles[1 - u // SLOTS, u % SLOTS]]
         mine.append(wanted)
         row = jnp.where(lane == u, wanted, row)
     req_v[0] = row
@@ -147,7 +148,7 @@
     def z_copy(way, step, c):
         sign = 1 - 2 * way
         index = (z - sign * step + NZ) % NZ
-        ref = slabs.at[index, pl.ds(c * GC, GC)]
+        ref = slabs.at[index, c // 2, pl.ds(c % 2 * GC, GC)]
         return pltpu.make_async_remote_copy(
             src_ref=ref, dst_ref=ref,
             send_sem=z_send.at[way, step, c], recv_sem=z_recv.at[way, step, c],
@@ -157,7 +158,7 @@
     def z_arrived(way, step, c):
         sign = 1 - 2 * way
         index = (z - sign * (step + 1) + NZ) % NZ
-        ref = slabs.at[index, pl.ds(c * GC, GC)]
+        ref = slabs.at[index, c // 2, pl.ds(c % 2 * GC, GC)]
         pltpu.make_async_remote_copy(
             src_ref=ref, dst_ref=ref,
             send_sem=z_send.at[way, step, c], recv_sem=z_recv.at[way, step, c],
@@ -174,6 +175,9 @@
 
     z_started = []
     for way, c in z_pieces(0):
+        if (way, c) == (0, CHUNKS // 2):
+            late.wait()
+            transform(1)
         copy = z_copy(way, 0, c)
         copy.start()
         z_started.append(copy)
@@ -233,7 +237,7 @@
     def first_hop(u):
         index, _ = asked(2, u)
         for s in (0, 1):
-            stage_a[u, s] = slabs[index, :, s]
+            stage_a[u, s] = slabs[index, s]
             copies["a", u, s] = send(
                 stage_a.at[u, s], got_x.at[u, s], a_send.at[u, s], a_recv.at[u, s],
                 at_y(1 if s == 0 else -1),
@@ -242,7 +246,7 @@
     def direct(u):
         for s, d, got in ((1, 1, got_p), (0, -1, got_m)):
             index, _ = asked(d % NY, u)
-            stage_d[u, s] = slabs[index, :, s]
+            stage_d[u, s] = slabs[index, s]
             copies["d", u, s] = send(
                 stage_d.at[u, s], got.at[u, s], d_send.at[u, s], d_recv.at[u, s], at_y(d)
             )
@@ -251,7 +255,7 @@
         for s, d, got in ((0, 1, got_p), (1, -1, got_m)):
             index, column = asked(d % NY, u)
             copies["a", u, s].wait_recv()
-            stage_m[u, s] = jnp.where(column == y, slabs[index, :, s], got_x[u, s])
+            stage_m[u, s] = jnp.where(column == y, slabs[index, s], got_x[u, s])
             copies["m", u, s] = send(
                 stage_m.at[u, s], got.at[u, s], m_send.at[u, s], m_recv.at[u, s], at_y(d)
             )
@@ -264,9 +268,9 @@
         up, down = (y + 1) % NY, (y + NY - 1) % NY
         own = column == y
         low = jnp.where(column == up, got_m[u, 0], got_p[u, 0])
-        low = jnp.where(own, slabs[index, :, 0], low)
+        low = jnp.where(own, slabs[index, 0], low)
         high = jnp.where(column == down, got_p[u, 1], got_m[u, 1])
-        high = jnp.where(own, slabs[index, :, 1], high)
+        high = jnp.where(own, slabs[index, 1], high)
         return low, high
 
     def send_first(k, value):
@@ -345,16 +349,15 @@
                 direct(u + 1)
         if u == 0:
             continue
-        k, role = (u - 1) // 2, (u - 1) % 2
         value = finish(u - 1)
-        if role == 0:
-            send_second(k, value)
-            if k > 0:
-                share_second(k - 1)
+        if u - 1 < SLOTS:
+            send_second(u - 1, value)
         else:
-            send_first(k, value)
-            pass_second(k)
-    share_second(SLOTS - 1)
+            send_first(u - 1 - SLOTS, value)
+        if 0 <= u - 2 < SLOTS:
+            pass_second(u - 2)
+        if 0 <= u - 3 < SLOTS:
+            share_second(u - 3)
     for k in range(SLOTS):
         close_second(k)
         copies["o", k].wait()
@@ -402,8 +405,8 @@
             pltpu.VMEM((rows, NT), F32),
             pltpu.VMEM((2 * NF, NT), BF),
             pltpu.VMEM((2 * NF, NT), BF),
-            dma((5,)),
-            pltpu.VMEM((NZ, NG, 2, 16, BLOCK), BF),
+            dma((6,)),
+            pltpu.VMEM((NZ, 2, NG, 16, BLOCK), BF),
             pltpu.VMEM((SLOTS, NG, 2, 16, BLOCK), BF),
             pltpu.VMEM(half_units, BF),
             pltpu.VMEM(half_units, BF),
@@ -464,7 +467,7 @@
             both = jnp.concatenate([direct, crossed], axis=1).astype(BF)
             halves.append(both.reshape(2 * NF, BLOCK))
         lhs = jnp.concatenate(halves, axis=1)
-        rhs = jnp.concatenate([b_ref[t, g, s] for s in (0, 1) for t in range(NTM)], axis=0)
+        rhs = jnp.concatenate([b_ref[k, t, g, s] for s in (0, 1) for t in range(NTM)], axis=0)
         cross = jnp.dot(lhs, rhs, preferred_element_type=F32).reshape(16, 16, BLOCK)
         rows = slice(g * 16, g * 16 + 16)
         top = cross.astype(BF)
@@ -492,8 +495,8 @@
         out_shape=jax.ShapeDtypeStruct((SLOTS, LAGS, share * BLOCK), F32),
         in_specs=[
             pl.BlockSpec(memory_space=pltpu.SMEM),
-            pl.BlockSpec((NTM, SLOTS, 2, 16, 2 * NF), lambda k: (0, 0, 0, 0, 0)),
-            pl.BlockSpec((None, NTM, NG, 2, 16, BLOCK), lambda k: (k, 0, 0, 0, 0, 0)),
+            pl.BlockSpec(memory_space=pltpu.VMEM),
+            pl.BlockSpec(memory_space=pltpu.VMEM),
             pl.BlockSpec((LAGS, 2 * NF), lambda k: (0, 0)),
             pl.BlockSpec((LAGS, 2 * NF), lambda k: (0, 0)),
         ],

time: 87.2 us -> 85.8 us (0.984)
  Pallas kernels: 86.4 us -> 84.9 us
    pallas_call x1, Pallas kernels: 79 us -> 77.5 us  [exchange(): pl.pallas_call(exchange_kernel, out_shape=(jax.ShapeDtypeStruct((SLOTS, N...]
where the time goes in v4:
time: 85.8 us; the launch traced here: 85.6 us
  Pallas kernels  84.9 us (99%)
    pallas_call x1, Pallas kernels, exchange(): pl.pallas_call(exchange_kernel, out_shape=(jax.ShapeDtypeStruct((SLOTS, N...  77.5 us
    pallas_call x1, Pallas kernels, stack(): pl.pallas_call(functools.partial(stack_kernel, scale), grid=(SLOTS,), out...  7.4 us

profile of v4, /device:TPU:1, one launch (start us, length us, event | category | flops | bytes accessed | tf_op | source)
XLA Modules:
  0.0 85.6 jit_solution(17557679019907127389)
XLA Ops:
  0.7 77.5 %exchange.1 = (bf16[3,8,16,2,16,128]{5,4,3,2,1,0:T(8,128)(2,1)S(1)}, bf16[8,3,2,16,256]{4,3,2,1,0:T(8,128)(2,1)S(1)}) custom-call(f32[256,1024]{1,0:T(8,128)} %bitcast.2, bf16[256,1024]{1,0:T(8,128)(2,1)} %constant.8.clone.hi_hbm, bf16[256,1024]{1,0:T(8,128)(2,1)} %constant.9.clone.lo_hbm, s32[64]{0:T(128)} %owner_hbm.1, s32[2,3]{1,0:T(2,128)} %bitcast.3), custom_call_target="tpu_custom_call" | custom-call | tf_op jit(solution)/shard_map/exchange/pallas_call | solution.py:394
  78.2 7.4 %stack.1 = f32[3,128,2048]{2,1,0:T(8,128)} custom-call(s32[1]{0:T(128)S(6)} %copy.9.counts, bf16[8,3,2,16,256]{4,3,2,1,0:T(8,128)(2,1)S(1)} %get-tuple-element.7.p_ref, bf16[3,8,16,2,16,128]{5,4,3,2,1,0:T(8,128)(2,1)S(1)} %get-tuple-element.8.b_ref, bf16[128,256]{1,0:T(8,128)(2,1)} %constant.10.clone.inv_hi, bf16[128,256]{1,0:T(8,128)(2,1)} %constant.11.clone.inv_lo), custom_call_target="tpu_custom_call" | custom-call | tf_op jit(solution)/shard_map/stack/pallas_call | solution.py:492

commit v5 on v4

--- a/solution.py
+++ b/solution.py
@@ -433,24 +433,30 @@
     )(*[in_hbm(a) for a in (traces.reshape(rows, NT), tab_hi, tab_lo, owner, tiles.T)])
 
 
-def stack_kernel(scale, counts, p_ref, b_ref, inv_hi, inv_lo, out, natural, first, turned, high, low):
-    k = pl.program_id(0)
-
-    @pl.when(k == 0)
-    def _():
-        eye = identity(2 * NF)
-        used = SLOTS * 32
-        pad = jnp.zeros((2 * NF, BLOCK - used), BF)
-        for t in range(NTM):
-            back = nt_dot(eye, p_ref[t].reshape(used, 2 * NF)).astype(BF)
-            natural[t] = jnp.concatenate([back, pad], axis=1)
-        eye = identity(BLOCK)
-        for g in range(NG):
-            tile = natural[:, g * 16 : (g + 1) * 16, :]
-            first[g] = nt_dot(eye, tile.reshape(BLOCK, BLOCK))
-            wide = tile.astype(F32)
-            wide = jnp.concatenate([-wide[:, 8:], wide[:, :8]], axis=1)
-            turned[g] = nt_dot(eye, wide.astype(BF).reshape(BLOCK, BLOCK))
+def stack_kernel(
+    scale, counts, p_ref, b_ref, hi_hbm, lo_hbm, out,
+    inv_hi, inv_lo, natural, first, turned, high, low, result, load_sem, out_sem,
+):
+    loads = [
+        pltpu.make_async_copy(hi_hbm, inv_hi, load_sem.at[0]),
+        pltpu.make_async_copy(lo_hbm, inv_lo, load_sem.at[1]),
+    ]
+    for load in loads:
+        load.start()
+
+    eye = identity(2 * NF)
+    used = SLOTS * 32
+    pad = jnp.zeros((2 * NF, BLOCK - used), BF)
+    for t in range(NTM):
+        back = nt_dot(eye, p_ref[t].reshape(used, 2 * NF)).astype(BF)
+        natural[t] = jnp.concatenate([back, pad], axis=1)
+    eye = identity(BLOCK)
+    for g in range(NG):
+        tile = natural[:, g * 16 : (g + 1) * 16, :]
+        first[g] = nt_dot(eye, tile.reshape(BLOCK, BLOCK))
+        wide = tile.astype(F32)
+        wide = jnp.concatenate([-wide[:, 8:], wide[:, :8]], axis=1)
+        turned[g] = nt_dot(eye, wide.astype(BF).reshape(BLOCK, BLOCK))
 
     shape = (8, BLOCK)
     mask = lax.broadcasted_iota(jnp.int32, shape, 1) % 8 == lax.broadcasted_iota(
@@ -458,10 +464,10 @@
     )
     mask = jnp.where(mask, 1.0, 0.0).astype(F32)[None]
 
-    def group(g):
+    def group(k, g):
         halves = []
         for s in (0, 1):
-            rows = pl.ds(pl.multiple_of(k * 32 + s * 16, 16), 16)
+            rows = slice(k * 32 + s * 16, k * 32 + s * 16 + 16)
             direct = first[g, rows, :][:, None, :] * mask
             crossed = turned[g, rows, :][:, None, :] * mask
             both = jnp.concatenate([direct, crossed], axis=1).astype(BF)
@@ -471,46 +477,58 @@
         cross = jnp.dot(lhs, rhs, preferred_element_type=F32).reshape(16, 16, BLOCK)
         rows = slice(g * 16, g * 16 + 16)
         top = cross.astype(BF)
-        high[:, rows, :] = top
-        low[:, rows, :] = (cross - top.astype(F32)).astype(BF)
-
-    for g in range(NG):
-        group(g)
-    factor = jnp.where(k < counts[0], scale, 0.0)
-    for i in range(0, 16, 2):
-        c_hi = jnp.concatenate([high[i], high[i + 1]], axis=1)
-        c_lo = jnp.concatenate([low[i], low[i + 1]], axis=1)
-        lagged = jnp.dot(inv_hi[...], c_hi, preferred_element_type=F32)
-        lagged = lagged + jnp.dot(inv_lo[...], c_hi, preferred_element_type=F32)
-        lagged = lagged + jnp.dot(inv_hi[...], c_lo, preferred_element_type=F32)
-        out[:, i * BLOCK : (i + 2) * BLOCK] = lagged * factor
+        high[k, :, rows, :] = top
+        low[k, :, rows, :] = (cross - top.astype(F32)).astype(BF)
+
+    copies = []
+    for k in range(SLOTS):
+        for g in range(NG):
+            group(k, g)
+        if k == 0:
+            for load in loads:
+                load.wait()
+        factor = jnp.where(k < counts[0], scale, 0.0)
+        for i in range(0, 16, 2):
+            c_hi = jnp.concatenate([high[k, i], high[k, i + 1]], axis=1)
+            c_lo = jnp.concatenate([low[k, i], low[k, i + 1]], axis=1)
+            lagged = jnp.dot(inv_hi[...], c_hi, preferred_element_type=F32)
+            lagged = lagged + jnp.dot(inv_lo[...], c_hi, preferred_element_type=F32)
+            lagged = lagged + jnp.dot(inv_hi[...], c_lo, preferred_element_type=F32)
+            result[k, :, i * BLOCK : (i + 2) * BLOCK] = lagged * factor
+            if i % 8 == 6:
+                lanes = pl.ds((i - 6) * BLOCK, 8 * BLOCK)
+                copy = pltpu.make_async_copy(
+                    result.at[k, :, lanes], out.at[k, :, lanes], out_sem.at[k, i // 8]
+                )
+                copy.start()
+                copies.append(copy)
+    for copy in copies:
+        copy.wait()
 
 
 def stack(counts, p_all, b_all, scale):
     inv_hi, inv_lo = inverse_table()
     share = BLOCK // NTM
+    vmem = pl.BlockSpec(memory_space=pltpu.VMEM)
+    hbm = pl.BlockSpec(memory_space=pltpu.HBM)
     return pl.pallas_call(
         functools.partial(stack_kernel, scale),
-        grid=(SLOTS,),
         out_shape=jax.ShapeDtypeStruct((SLOTS, LAGS, share * BLOCK), F32),
-        in_specs=[
-            pl.BlockSpec(memory_space=pltpu.SMEM),
-            pl.BlockSpec(memory_space=pltpu.VMEM),
-            pl.BlockSpec(memory_space=pltpu.VMEM),
-            pl.BlockSpec((LAGS, 2 * NF), lambda k: (0, 0)),
-            pl.BlockSpec((LAGS, 2 * NF), lambda k: (0, 0)),
-        ],
-        out_specs=pl.BlockSpec((None, LAGS, share * BLOCK), lambda k: (k, 0, 0)),
+        in_specs=[pl.BlockSpec(memory_space=pltpu.SMEM), vmem, vmem, hbm, hbm],
+        out_specs=hbm,
         scratch_shapes=[
+            pltpu.VMEM((LAGS, 2 * NF), BF),
+            pltpu.VMEM((LAGS, 2 * NF), BF),
             pltpu.VMEM((NTM, 2 * NF, BLOCK), BF),
             pltpu.VMEM((NG, BLOCK, BLOCK), F32),
             pltpu.VMEM((NG, BLOCK, BLOCK), F32),
-            pltpu.VMEM((16, 2 * NF, BLOCK), BF),
-            pltpu.VMEM((16, 2 * NF, BLOCK), BF),
+            pltpu.VMEM((SLOTS, 16, 2 * NF, BLOCK), BF),
+            pltpu.VMEM((SLOTS, 16, 2 * NF, BLOCK), BF),
+            pltpu.VMEM((SLOTS, LAGS, share * BLOCK), F32),
+            pltpu.SemaphoreType.DMA((2,)),
+            pltpu.SemaphoreType.DMA((SLOTS, 2)),
         ],
-        compiler_params=pltpu.CompilerParams(
-            dimension_semantics=("arbitrary",), vmem_limit_bytes=32 << 20
-        ),
+        compiler_params=pltpu.CompilerParams(vmem_limit_bytes=32 << 20),
         name="stack",
     )(counts, p_all, b_all, in_hbm(inv_hi), in_hbm(inv_lo))
 

time: 85.8 us -> 84.1 us (0.980)
  Pallas kernels: 84.9 us -> 83.3 us
    pallas_call x1, Pallas kernels: 7.4 us -> 5.73 us  [stack(): pl.pallas_call(functools.partial(stack_kernel, scale), out_shape=jax.Shap...]
where the time goes in v5:
time: 84.1 us; the launch traced here: 83.9 us
  Pallas kernels  83.3 us (99%)
    pallas_call x1, Pallas kernels, exchange(): pl.pallas_call(exchange_kernel, out_shape=(jax.ShapeDtypeStruct((SLOTS, N...  77.5 us
    pallas_call x1, Pallas kernels, stack(): pl.pallas_call(functools.partial(stack_kernel, scale), out_shape=jax.Shap...  5.73 us

profile of v5, /device:TPU:1, one launch (start us, length us, event | category | flops | bytes accessed | tf_op | source)
XLA Modules:
  0.0 83.9 jit_solution(12227783154199395485)
XLA Ops:
  0.7 77.5 %exchange.1 = (bf16[3,8,16,2,16,128]{5,4,3,2,1,0:T(8,128)(2,1)S(1)}, bf16[8,3,2,16,256]{4,3,2,1,0:T(8,128)(2,1)S(1)}) custom-call(f32[256,1024]{1,0:T(8,128)} %bitcast.2, bf16[256,1024]{1,0:T(8,128)(2,1)} %constant.8.clone.hi_hbm, bf16[256,1024]{1,0:T(8,128)(2,1)} %constant.9.clone.lo_hbm, s32[64]{0:T(128)} %owner_hbm.1, s32[2,3]{1,0:T(2,128)} %bitcast.3), custom_call_target="tpu_custom_call" | custom-call | tf_op jit(solution)/shard_map/exchange/pallas_call | solution.py:394
  78.2 5.7 %stack.1 = f32[3,128,2048]{2,1,0:T(8,128)} custom-call(s32[1]{0:T(128)S(6)} %copy.9.counts, bf16[8,3,2,16,256]{4,3,2,1,0:T(8,128)(2,1)S(1)} %get-tuple-element.7.p_ref, bf16[3,8,16,2,16,128]{5,4,3,2,1,0:T(8,128)(2,1)S(1)} %get-tuple-element.8.b_ref, bf16[128,256]{1,0:T(8,128)(2,1)} %constant.10.clone.hi_hbm, bf16[128,256]{1,0:T(8,128)(2,1)} %constant.11.clone.lo_hbm), custom_call_target="tpu_custom_call" | custom-call | tf_op jit(solution)/shard_map/stack/pallas_call | solution.py:514

commit v6 on v5

--- a/solution.py
+++ b/solution.py
@@ -68,7 +68,7 @@
     traces_hbm, hi_hbm, lo_hbm, owner_hbm, tiles_hbm, b_out, p_out,
     owner, tiles, traces, tab_hi, tab_lo, load_sem, slabs, picks, stage_a, stage_d, stage_m, got_x, got_p, got_m,
     packed, req_v, req_s,
-    z_send, z_recv, r_send, r_recv, r_loc, a_send, a_recv, d_send, d_recv, m_send, m_recv,
+    z_send, z_recv, r_send, r_recv, r_loc, a_send, a_recv, m_send, m_recv,
     b_send, b_recv, p_send, p_recv, own_sem,
 ):
     t = lax.axis_index("tm")
@@ -243,27 +243,19 @@
                 at_y(1 if s == 0 else -1),
             )
 
-    def direct(u):
-        for s, d, got in ((1, 1, got_p), (0, -1, got_m)):
-            index, _ = asked(d % NY, u)
-            stage_d[u, s] = slabs[index, s]
-            copies["d", u, s] = send(
-                stage_d.at[u, s], got.at[u, s], d_send.at[u, s], d_recv.at[u, s], at_y(d)
-            )
-
-    def merged(u):
-        for s, d, got in ((0, 1, got_p), (1, -1, got_m)):
+    def second_hop(u):
+        for s, d, stage, got in ((0, 1, stage_d, got_p), (1, -1, stage_m, got_m)):
             index, column = asked(d % NY, u)
+            stage[u, 1 - s] = slabs[index, 1 - s]
             copies["a", u, s].wait_recv()
-            stage_m[u, s] = jnp.where(column == y, slabs[index, s], got_x[u, s])
+            stage[u, s] = jnp.where(column == y, slabs[index, s], got_x[u, s])
             copies["m", u, s] = send(
-                stage_m.at[u, s], got.at[u, s], m_send.at[u, s], m_recv.at[u, s], at_y(d)
+                stage.at[u], got.at[u], m_send.at[u, s], m_recv.at[u, s], at_y(d)
             )
 
     def finish(u):
         index, column = asked(0, u)
         for s in (0, 1):
-            copies["d", u, s].wait_recv()
             copies["m", u, s].wait_recv()
         up, down = (y + 1) % NY, (y + NY - 1) % NY
         own = column == y
@@ -339,14 +331,12 @@
 
     first_hop(0)
     first_hop(1)
-    direct(0)
+    first_hop(2)
     for u in range(UNITS + 1):
         if u < UNITS:
-            merged(u)
-            if u + 2 < UNITS:
-                first_hop(u + 2)
-            if u + 1 < UNITS:
-                direct(u + 1)
+            second_hop(u)
+            if u + 3 < UNITS:
+                first_hop(u + 3)
         if u == 0:
             continue
         value = finish(u - 1)
@@ -374,7 +364,7 @@
         copy.wait_send()
     for u in range(UNITS):
         for s in (0, 1):
-            for kind in ("a", "d", "m"):
+            for kind in ("a", "m"):
                 copies[kind, u, s].wait_send()
     for k in range(SLOTS):
         for d in range(1, NTM):
@@ -421,7 +411,6 @@
             dma((NY,)), dma((NY,)), dma((NY,)),
             dma((UNITS, 2)), dma((UNITS, 2)),
             dma((UNITS, 2)), dma((UNITS, 2)),
-            dma((UNITS, 2)), dma((UNITS, 2)),
             dma((SLOTS, 9)), dma((SLOTS, 9)),
             dma((SLOTS, NTM)), dma((SLOTS, NTM)),
             dma((2 * SLOTS,)),

time: 84.1 us -> 85.3 us (1.014)
  Pallas kernels: 83.3 us -> 84.5 us
    pallas_call x1, Pallas kernels: 77.5 us -> 78.7 us  [exchange(): pl.pallas_call(exchange_kernel, out_shape=(jax.ShapeDtypeStruct((SLOTS, N...]
where the time goes in v6:
time: 85.3 us; the launch traced here: 85.1 us
  Pallas kernels  84.5 us (99%)
    pallas_call x1, Pallas kernels, exchange(): pl.pallas_call(exchange_kernel, out_shape=(jax.ShapeDtypeStruct((SLOTS, N...  78.7 us
    pallas_call x1, Pallas kernels, stack(): pl.pallas_call(functools.partial(stack_kernel, scale), out_shape=jax.Shap...  5.73 us

profile of v6, /device:TPU:1, one launch (start us, length us, event | category | flops | bytes accessed | tf_op | source)
XLA Modules:
  0.0 85.1 jit_solution(12205318482379280757)
XLA Ops:
  0.7 78.7 %exchange.1 = (bf16[3,8,16,2,16,128]{5,4,3,2,1,0:T(8,128)(2,1)S(1)}, bf16[8,3,2,16,256]{4,3,2,1,0:T(8,128)(2,1)S(1)}) custom-call(f32[256,1024]{1,0:T(8,128)} %bitcast.2, bf16[256,1024]{1,0:T(8,128)(2,1)} %constant.8.clone.hi_hbm, bf16[256,1024]{1,0:T(8,128)(2,1)} %constant.9.clone.lo_hbm, s32[64]{0:T(128)} %owner_hbm.1, s32[2,3]{1,0:T(2,128)} %bitcast.3), custom_call_target="tpu_custom_call" | custom-call | tf_op jit(solution)/shard_map/exchange/pallas_call | solution.py:384
  79.4 5.7 %stack.1 = f32[3,128,2048]{2,1,0:T(8,128)} custom-call(s32[1]{0:T(128)S(6)} %copy.9.counts, bf16[8,3,2,16,256]{4,3,2,1,0:T(8,128)(2,1)S(1)} %get-tuple-element.7.p_ref, bf16[3,8,16,2,16,128]{5,4,3,2,1,0:T(8,128)(2,1)S(1)} %get-tuple-element.8.b_ref, bf16[128,256]{1,0:T(8,128)(2,1)} %constant.10.clone.hi_hbm, bf16[128,256]{1,0:T(8,128)(2,1)} %constant.11.clone.lo_hbm), custom_call_target="tpu_custom_call" | custom-call | tf_op jit(solution)/shard_map/stack/pallas_call | solution.py:503

commit v7 on v5

--- a/solution.py
+++ b/solution.py
@@ -22,7 +22,7 @@
 NTM = 8
 SLOTS = 3
 UNITS = 2 * SLOTS
-CHUNKS = 4
+CHUNKS = 8
 GC = 2 * NG // CHUNKS
 BF = jnp.bfloat16
 F32 = jnp.float32
@@ -148,7 +148,7 @@
     def z_copy(way, step, c):
         sign = 1 - 2 * way
         index = (z - sign * step + NZ) % NZ
-        ref = slabs.at[index, c // 2, pl.ds(c % 2 * GC, GC)]
+        ref = slabs.at[index, c * GC // NG, pl.ds(c * GC % NG, GC)]
         return pltpu.make_async_remote_copy(
             src_ref=ref, dst_ref=ref,
             send_sem=z_send.at[way, step, c], recv_sem=z_recv.at[way, step, c],
@@ -158,7 +158,7 @@
     def z_arrived(way, step, c):
         sign = 1 - 2 * way
         index = (z - sign * (step + 1) + NZ) % NZ
-        ref = slabs.at[index, c // 2, pl.ds(c % 2 * GC, GC)]
+        ref = slabs.at[index, c * GC // NG, pl.ds(c * GC % NG, GC)]
         pltpu.make_async_remote_copy(
             src_ref=ref, dst_ref=ref,
             send_sem=z_send.at[way, step, c], recv_sem=z_recv.at[way, step, c],

time: 84.1 us -> 83.6 us (level)
  no operation moved by 1% of the time
where the time goes in v7:
time: 83.6 us; the launch traced here: 83.4 us
  Pallas kernels  82.8 us (99%)
    pallas_call x1, Pallas kernels, exchange(): pl.pallas_call(exchange_kernel, out_shape=(jax.ShapeDtypeStruct((SLOTS, N...  77 us
    pallas_call x1, Pallas kernels, stack(): pl.pallas_call(functools.partial(stack_kernel, scale), out_shape=jax.Shap...  5.73 us

profile of v7, /device:TPU:1, one launch (start us, length us, event | category | flops | bytes accessed | tf_op | source)
XLA Modules:
  0.0 83.4 jit_solution(8684418479204048874)
XLA Ops:
  0.7 77.0 %exchange.1 = (bf16[3,8,16,2,16,128]{5,4,3,2,1,0:T(8,128)(2,1)S(1)}, bf16[8,3,2,16,256]{4,3,2,1,0:T(8,128)(2,1)S(1)}) custom-call(f32[256,1024]{1,0:T(8,128)} %bitcast.2, bf16[256,1024]{1,0:T(8,128)(2,1)} %constant.8.clone.hi_hbm, bf16[256,1024]{1,0:T(8,128)(2,1)} %constant.9.clone.lo_hbm, s32[64]{0:T(128)} %owner_hbm.1, s32[2,3]{1,0:T(2,128)} %bitcast.3), custom_call_target="tpu_custom_call" | custom-call | tf_op jit(solution)/shard_map/exchange/pallas_call | solution.py:394
  77.7 5.7 %stack.1 = f32[3,128,2048]{2,1,0:T(8,128)} custom-call(s32[1]{0:T(128)S(6)} %copy.9.counts, bf16[8,3,2,16,256]{4,3,2,1,0:T(8,128)(2,1)S(1)} %get-tuple-element.7.p_ref, bf16[3,8,16,2,16,128]{5,4,3,2,1,0:T(8,128)(2,1)S(1)} %get-tuple-element.8.b_ref, bf16[128,256]{1,0:T(8,128)(2,1)} %constant.10.clone.hi_hbm, bf16[128,256]{1,0:T(8,128)(2,1)} %constant.11.clone.lo_hbm), custom_call_target="tpu_custom_call" | custom-call | tf_op jit(solution)/shard_map/stack/pallas_call | solution.py:514
